TPU v7x, 512 devices: a whole 4x8x8 slice. The times are simulated.
512 devices in a mesh: items: 32 (over x, y), cents: 16 (over z, core).
Axes of the slice: x: 4, y: 8, z: 8, core: 2. Of those that a mesh axis runs over, the one named last changes fastest.
Arguments:
- embeddings: bfloat16 [61440, 1024], P('items')
- counts: int32 [32], P('items'), may hold values from 1152 to 1920, as said below
- centroids: bfloat16 [2048, 1024], P('cents')
Outputs:
- final_centroids: bfloat16 [2048, 1024], P('cents')
Inputs may be any that keep to these rules, and one draw needn't show every extreme that they name: The counts of replicas 0 to i-1 sum to 1536 * i plus an offset of at most 192 in either direction, reached both ways in every draw; all counts sum to 49152. Rows of a buffer past its count carry no data.
All inputs are finite; a program needn't handle non-finite values.
Results may differ from a plain program's by a relative error of at most 0.0112.
Values may be sent and summed in bfloat16 or wider, within the bound.
No kernel may reach another device: no remote copies, remote signals or barrier semaphores. Data moves between devices by JAX's collectives and lax.ppermute only.
A program may use at most 64 MiB of HBM per device.

v0:
```python
import jax
import jax.numpy as jnp
from jax import lax
from jax.sharding import PartitionSpec as P

D = 1024
ROWS_DEV = 1536
ITERS = 2
SPILL = 192


prior_count = 2.0


def prefix(part, axis, combine, identity):
    place = lax.axis_index(axis)
    gathered = lax.all_gather(part, axis)
    state = jnp.zeros_like(part) + jnp.asarray(identity, part.dtype)

    def one(hop, state):
        return combine(state, lax.dynamic_index_in_dim(gathered, hop, 0, False))

    return lax.fori_loop(0, place, one, state)


def with_halo(block, sides, width):
    for axis, dim in sides:
        count = lax.axis_size(axis)
        forward = [(i, i + 1) for i in range(count - 1)]
        backward = [(target, source) for source, target in forward]
        low = lax.ppermute(
            lax.slice_in_dim(block, block.shape[dim] - width, None, axis=dim), axis, forward
        )
        high = lax.ppermute(lax.slice_in_dim(block, 0, width, axis=dim), axis, backward)
        block = jnp.concatenate([low, block, high], axis=dim)
    return block


def add_counts(earlier, later):
    return earlier + later


def settle_rows(embeddings, counts):
    capacity = embeddings.shape[0]
    own_count = counts[0]
    position = lax.axis_index("items")
    before = prefix(counts, "items", add_counts, jnp.zeros((1,), jnp.int32))[0]
    excess_below = before - position * ROWS_DEV
    excess_here = excess_below + own_count - ROWS_DEV
    from_below = jnp.maximum(excess_below, 0)
    sent_down = jnp.maximum(-excess_below, 0)
    from_above = jnp.maximum(-excess_here, 0)
    tail_rows = lax.dynamic_slice_in_dim(embeddings, own_count - SPILL, SPILL, 0)
    edge_rows = jnp.concatenate([embeddings[:SPILL], tail_rows], axis=0)
    extended = with_halo(edge_rows, (("items", 0),), SPILL)
    lower_rows = extended[:SPILL]
    upper_rows = extended[3 * SPILL :]
    joined = jnp.concatenate([lower_rows, embeddings, upper_rows], axis=0)
    slot_ids = jnp.arange(ROWS_DEV, dtype=jnp.int32)
    kept_rows = ROWS_DEV - from_below - from_above
    source = jnp.where(
        slot_ids < from_below,
        SPILL - from_below + slot_ids,
        jnp.where(
            slot_ids < from_below + kept_rows,
            SPILL + sent_down + slot_ids - from_below,
            SPILL + capacity + slot_ids - from_below - kept_rows,
        ),
    )
    return jnp.take(joined, source, axis=0)


def body(embeddings, counts, centroids):
    settled = settle_rows(embeddings, counts)
    scale = D ** (-0.5)
    current = centroids
    for step in range(ITERS):
        cent_f = current.astype(jnp.float32)
        norms = jnp.sum(cent_f * cent_f, axis=1)
        dots = lax.dot_general(
            settled, current, (((1,), (1,)), ((), ())), preferred_element_type=jnp.float32
        )
        score = (2.0 * dots - norms[None, :]) * scale
        top = lax.pmax(jnp.max(score, axis=1), "cents")
        expo = jnp.exp(score - top[:, None])
        total = lax.psum(jnp.sum(expo, axis=1), "cents")
        resp = (expo / total[:, None]).astype(jnp.bfloat16)
        mass_here = jnp.sum(resp.astype(jnp.float32), axis=0)
        moment_here = lax.dot_general(
            resp, settled, (((0,), (0,)), ((), ())), preferred_element_type=jnp.float32
        )
        moment, mass = lax.psum((moment_here, mass_here), "items")
        current = ((moment + prior_count * cent_f) / (mass[:, None] + prior_count)).astype(
            jnp.bfloat16
        )
    return current


def solution(mesh):
    in_specs = (P("items", None), P("items"), P("cents", None))
    out_specs = P("cents", None)
    return jax.shard_map(body, mesh=mesh, in_specs=in_specs, out_specs=out_specs, check_vma=False)
```

profile of v0, /device:TPU:8, one launch (start us, length us, event | category | flops | bytes accessed | tf_op | source)
XLA Modules:
  0.0 527.0 jit_solution(12058598038848635442)
XLA Ops:
  7.2 1.3 constant_dynamic-slice_fusion.1
  8.5 3.5 collective-permute-start
  12.0 5.6 %collective-permute-start.1 = (bf16[192,1024]{1,0:T(8,128)(2,1)S(1)}, bf16[192,1024]{1,0:T(8,128)(2,1)S(1)}, u32[]{:S(2)}, u32[]{:S(2)}) collective-permute-start(bf16[192,1024]{1,0:T(8,128)(2,1)S(1)} %get-tuple-element.44), channel_id=1, source_target_pairs={{16,0},{32,16},{48,32},{64,48},{80,64},{96,80},{112,96},{128,112},... | collective-permute-start | bytes 1179656 | tf_op jit(solution)/shard_map/ppermute | solution.py:34
  17.5 1.3 dynamic-slice
  18.9 0.7 dynamic-update-slice
  19.6 18.1 %all-reduce = s32[32]{0:T(128)S(1)} all-reduce(s32[32]{0:T(128)S(1)} %dynamic-update-slice), channel_id=2, replica_groups=mesh['items'=32,'cents'=16] {'items'}, use_global_device_ids=true, to_apply=%add | all-reduce | flops 32 | bytes 256
  37.7 1.3 while.10
  37.7 0.6 constant_dynamic-slice_fusion.3
  39.1 1.1 fusion.6
  40.2 3.9 pad_maximum_fusion
  44.2 10.8 %gather_fusion = bf16[1536,1024]{1,0:T(8,128)(2,1)} fusion(bf16[2304,1024]{1,0:T(8,128)(2,1)} %pad_maximum_fusion, s32[2048]{0:T(1024)S(1)} %pad_clamp_fusion), kind=kCustom, calls=%fused_computation | custom fusion | bytes 6297600 | tf_op jit(solution)/shard_map/jit(_take)/gather | solution.py:70
  54.9 3.2 fusion.18
  58.1 29.7 %pmax.14 = f32[1536]{0:T(1024)S(1)} all-reduce(f32[1536]{0:T(1024)S(1)} %get-tuple-element.45), channel_id=1, replica_groups=mesh['items'=32,'cents'=16] {'cents'}, use_global_device_ids=true, to_apply=%region_4.5 | all-reduce | flops 1536 | bytes 12288 | tf_op jit(solution)/shard_map/pmax | solution.py:84
  87.9 0.1 fusion.4
  88.0 24.4 %psum.42 = f32[1536]{0:T(1024)S(1)} all-reduce(f32[1536]{0:T(1024)S(1)} %fusion.4), channel_id=1, replica_groups=mesh['items'=32,'cents'=16] {'cents'}, use_global_device_ids=true, to_apply=%region_6.7 | all-reduce | flops 1536 | bytes 12288 | tf_op jit(solution)/shard_map/psum | solution.py:86
  112.4 0.2 convert_reduce_fusion.1
  112.6 3.4 fusion.16
  116.1 0.0 all-reduce.4.cloned.1.call-update
  116.1 0.0 all-reduce.6.cloned.1.call-start
  116.1 107.1 %psum.44 = f32[128]{0:T(128)S(1)} all-reduce(f32[128]{0:T(128)S(1)} %get-tuple-element.41), channel_id=1, replica_groups=mesh['items'=32,'cents'=16] {'items'}, use_global_device_ids=true, to_apply=%region_9.10 | all-reduce | flops 128 | bytes 1024 | tf_op jit(solution)/shard_map/psum | solution.py:92
  223.2 83.0 %all-reduce.4.cloned.1.call-done = f32[128,1024]{1,0:T(8,128)} async-done(((f32[128,1024]{1,0:T(8,128)}), f32[128,1024]{1,0:T(8,128)}) %all-reduce.4.cloned.1.call-update) | async-done | bytes 524304 | tf_op jit(solution)/shard_map/psum | solution.py:92
  306.2 1.3 fusion.10
  307.5 3.2 fusion.19
  310.6 24.6 %pmax.15 = f32[1536]{0:T(1024)S(1)} all-reduce(f32[1536]{0:T(1024)S(1)} %get-tuple-element.47), channel_id=1, replica_groups=mesh['items'=32,'cents'=16] {'cents'}, use_global_device_ids=true, to_apply=%region_12.13 | all-reduce | flops 1536 | bytes 12288 | tf_op jit(solution)/shard_map/pmax | solution.py:84
  335.3 0.1 fusion.5
  335.4 24.4 %psum.45 = f32[1536]{0:T(1024)S(1)} all-reduce(f32[1536]{0:T(1024)S(1)} %fusion.5), channel_id=1, replica_groups=mesh['items'=32,'cents'=16] {'cents'}, use_global_device_ids=true, to_apply=%region_14.15 | all-reduce | flops 1536 | bytes 12288 | tf_op jit(solution)/shard_map/psum | solution.py:86
  359.8 0.2 convert_reduce_fusion
  360.1 3.4 fusion.15
  363.5 0.0 all-reduce.6.cloned.1.call-update
  363.5 71.1 %psum.47 = f32[128]{0:T(128)S(1)} all-reduce(f32[128]{0:T(128)S(1)} %get-tuple-element.37), channel_id=1, replica_groups=mesh['items'=32,'cents'=16] {'items'}, use_global_device_ids=true, to_apply=%region_17.18 | all-reduce | flops 128 | bytes 1024 | tf_op jit(solution)/shard_map/psum | solution.py:92
  434.6 83.7 %all-reduce.6.cloned.1.call-done = f32[128,1024]{1,0:T(8,128)} async-done(((f32[128,1024]{1,0:T(8,128)}), f32[128,1024]{1,0:T(8,128)}) %all-reduce.6.cloned.1.call-update) | async-done | bytes 524304 | tf_op jit(solution)/shard_map/psum | solution.py:92
  518.3 1.9 fusion.13
  (11 shorter events, 0.1 us)
Async XLA Ops:
  6.5 299.7 %all-reduce.4.cloned.1.call-start = ((), (), s32[]{:S(2)}) async-start(), calls=%async_computation | async-start | bytes 1048576 | tf_op jit(solution)/shard_map/psum | solution.py:92
  8.5 31.8 %collective-permute-start = (bf16[192,1024]{1,0:T(8,128)(2,1)S(1)}, bf16[192,1024]{1,0:T(8,128)(2,1)S(1)}, u32[]{:S(2)}, u32[]{:S(2)}) collective-permute-start(bf16[192,1024]{1,0:T(8,128)(2,1)S(1)} %get-tuple-element.43), channel_id=1, source_target_pairs={{0,16},{16,32},{32,48},{48,64},{64,80},{80,96},{96,112},{112,128},... | collective-permute-start | bytes 1179656 | tf_op jit(solution)/shard_map/ppermute | solution.py:31
  12.0 28.3 %collective-permute-start.1 = (bf16[192,1024]{1,0:T(8,128)(2,1)S(1)}, bf16[192,1024]{1,0:T(8,128)(2,1)S(1)}, u32[]{:S(2)}, u32[]{:S(2)}) collective-permute-start(bf16[192,1024]{1,0:T(8,128)(2,1)S(1)} %get-tuple-element.44), channel_id=1, source_target_pairs={{16,0},{32,16},{48,32},{64,48},{80,64},{96,80},{112,96},{128,112},... | collective-permute-start | bytes 1179656 | tf_op jit(solution)/shard_map/ppermute | solution.py:34
  44.2 10.8 %copy-start = (bf16[128,1024]{1,0:T(8,128)(2,1)S(1)}, bf16[128,1024]{1,0:T(8,128)(2,1)}, u32[]{:S(2)}) copy-start(bf16[128,1024]{1,0:T(8,128)(2,1)} %param.7) | copy-start | bytes 786436
  116.1 402.2 %all-reduce.6.cloned.1.call-start = ((), (), s32[]{:S(2)}) async-start(), calls=%async_computation.1 | async-start | bytes 1048576 | tf_op jit(solution)/shard_map/psum | solution.py:92
Sparse Core Ops, SparseCore 0:
  116.2 189.9 all-reduce.3
  363.6 154.6 all-reduce.5
where the time goes:
time: 528 us; the launch traced here: 527 us
  blocking collectives  300 us (57%)
  waiting for transfers between devices  167 us (32%)
  local copies, waits for them, and re-layouts  14.7 us (3%)
  between operations  14.2 us (3%)
  matrix products  13.2 us (2%)
  starting transfers between devices  9.09 us (2%)
  other arithmetic  8.94 us (2%)
    psum x2, blocking collectives, body(): moment, mass = lax.psum((moment_here, mass_here), 'items')  178 us
    psum x2, waiting for transfers between devices, body(): moment, mass = lax.psum((moment_here, mass_here), 'items')  167 us
    pmax x2, blocking collectives, body(): top = lax.pmax(jnp.max(score, axis=1), 'cents')  54.4 us
    psum x2, blocking collectives, body(): total = lax.psum(jnp.sum(expo, axis=1), 'cents')  48.8 us
    unnamed x1, blocking collectives  18.1 us
    gather x1, local copies, waits for them, and re-layouts, settle_rows(): return jnp.take(joined, source, axis=0)  10.8 us
  transfers between devices with their start and end apart: 4, of which 2 were waited for; matrix products, arithmetic and copies ran while one was open for 1% of the time, Pallas kernels for 0%

commit v1 on v0

v1 whole, which is shorter than its diff:
```python
import jax
import jax.numpy as jnp
from jax import lax
from jax.sharding import PartitionSpec as P

D = 1024
ITERS = 2
prior_count = 2.0


def gather_all(part, axis):
    count = lax.axis_size(axis)
    return lax.all_to_all(jnp.broadcast_to(part[None], (count,) + part.shape), axis, 0, 0)


def body(embeddings, counts, centroids):
    rows = embeddings.shape[0]
    cents = centroids.shape[0]
    n_items = lax.axis_size("items")
    own = cents // n_items
    place = lax.axis_index("items")
    scale = D ** (-0.5)
    valid = jnp.arange(rows, dtype=jnp.int32) < counts[0]
    current = centroids
    for step in range(ITERS):
        cent_f = current.astype(jnp.float32)
        norms = jnp.sum(cent_f * cent_f, axis=1)
        dots = lax.dot_general(
            current, embeddings, (((1,), (1,)), ((), ())), preferred_element_type=jnp.float32
        )
        score = (2.0 * dots - norms[:, None]) * scale
        top = jnp.max(score, axis=0)
        logs = top + jnp.log(jnp.sum(jnp.exp(score - top[None]), axis=0))
        all_logs = gather_all(logs, "cents")
        high = jnp.max(all_logs, axis=0)
        total = high + jnp.log(jnp.sum(jnp.exp(all_logs - high[None]), axis=0))
        resp = jnp.where(valid[None], jnp.exp(score - total[None]), 0.0).astype(jnp.bfloat16)
        mass = jnp.sum(resp.astype(jnp.float32), axis=1)
        moment = lax.dot_general(
            resp, embeddings, (((1,), (0,)), ((), ())), preferred_element_type=jnp.float32
        )
        mass_high = mass.astype(jnp.bfloat16)
        mass_low = (mass - mass_high.astype(jnp.float32)).astype(jnp.bfloat16)
        lanes = lax.broadcasted_iota(jnp.int32, (cents, 128), 1)
        masses = jnp.where(lanes == 0, mass_high[:, None], mass_low[:, None])
        sent = jnp.concatenate([moment.astype(jnp.bfloat16), masses], axis=1)
        parts = lax.all_to_all(sent.reshape(n_items, own, D + 128), "items", 0, 0)
        sums = jnp.sum(parts.astype(jnp.float32), axis=0)
        own_mass = sums[:, D] + sums[:, D + 1]
        before = lax.dynamic_slice_in_dim(current, place * own, own, 0).astype(jnp.float32)
        fresh = (sums[:, :D] + prior_count * before) / (own_mass[:, None] + prior_count)
        current = gather_all(fresh.astype(jnp.bfloat16), "items").reshape(cents, D)
    return current


def solution(mesh):
    in_specs = (P("items", None), P("items"), P("cents", None))
    out_specs = P("cents", None)
    return jax.shard_map(body, mesh=mesh, in_specs=in_specs, out_specs=out_specs, check_vma=False)
```

time: 528 us -> 126 us (0.24)
  blocking collectives: 300 us -> 62.9 us
  waiting for transfers between devices: 167 us -> 21.8 us
  between operations: 14.2 us -> 0.86 us
  local copies, waits for them, and re-layouts: 14.7 us -> 2.72 us
  starting transfers between devices: 9.09 us -> 20.6 us
    psum x4 -> x0, blocking collectives: 227 us -> none  [the longest x2 178 us: body(): moment, mass = lax.psum((moment_here, mass_here), 'items')]
    psum x2 -> x0, waiting for transfers between devices: 167 us -> none  [body(): moment, mass = lax.psum((moment_here, mass_here), 'items')]
    all_to_all x0 -> x4, blocking collectives: none -> 62.9 us  [the longest x3 44.7 us: gather_all(): lax.all_to_all(jnp.broadcast_to(part[None], (count,) + part.shape), axis,...]
    pmax x2 -> x0, blocking collectives: 54.4 us -> none  [body(): top = lax.pmax(jnp.max(score, axis=1), 'cents')]
    all_to_all x0 -> x2, waiting for transfers between devices: none -> 21.8 us  [the longest x1 13.9 us: body(): parts = lax.all_to_all(sent.reshape(n_items, own, D + 128), 'items', 0, 0)]
    all_to_all x0 -> x2, starting transfers between devices: none -> 20.6 us  [the longest x1 10.4 us: gather_all(): lax.all_to_all(jnp.broadcast_to(part[None], (count,) + part.shape), axis,...]
    unnamed x1 -> x0, blocking collectives: 18.1 us -> none
    gather x1 -> x0, local copies, waits for them, and re-layouts: 10.8 us -> none  [settle_rows(): return jnp.take(joined, source, axis=0)]
  transfers between devices with their start and end apart: 4 -> 2, of which waited for: 2 -> 2; matrix products, arithmetic and copies ran while one was open for 1% -> 0% of each run, Pallas kernels for 0% -> 0%
where the time goes in v1:
time: 126 us
  blocking collectives  62.9 us (50%)
  waiting for transfers between devices  21.8 us (17%)
  starting transfers between devices  20.6 us (16%)
  matrix products  12.8 us (10%)
  other arithmetic  4.17 us (3%)
  local copies, waits for them, and re-layouts  2.72 us (2%)
    all_to_all x3, blocking collectives, gather_all(): lax.all_to_all(jnp.broadcast_to(part[None], (count,) + part.shape), axis,...  44.7 us
    all_to_all x1, blocking collectives, body(): parts = lax.all_to_all(sent.reshape(n_items, own, D + 128), 'items', 0, 0)  18.2 us
    all_to_all x1, waiting for transfers between devices, body(): parts = lax.all_to_all(sent.reshape(n_items, own, D + 128), 'items', 0, 0)  13.9 us
    all_to_all x1, starting transfers between devices, gather_all(): lax.all_to_all(jnp.broadcast_to(part[None], (count,) + part.shape), axis,...  10.4 us
    all_to_all x1, starting transfers between devices, body(): parts = lax.all_to_all(sent.reshape(n_items, own, D + 128), 'items', 0, 0)  10.2 us
    all_to_all x1, waiting for transfers between devices, gather_all(): lax.all_to_all(jnp.broadcast_to(part[None], (count,) + part.shape), axis,...  7.93 us
    dot_general x2, matrix products, body(): lax.dot_general(current, embeddings, (((1,), (1,)), ((), ())), preferred_...  7.11 us
    dot_general x2, matrix products, body(): lax.dot_general(resp, embeddings, (((1,), (0,)), ((), ())), preferred_ele...  5.67 us
  transfers between devices with their start and end apart: 2, of which 2 were waited for; matrix products, arithmetic and copies ran while one was open for 0% of the time, Pallas kernels for 0%

profile of v1, /device:TPU:8, one launch (start us, length us, event | category | flops | bytes accessed | tf_op | source)
XLA Modules:
  0.0 125.8 jit_solution(6260709879010516227)
XLA Ops:
  0.0 1.1 multiply_reduce_fusion.1
  1.1 3.6 %fusion.20 = (f32[1920]{0:T(1024)S(1)}, f32[128,1920]{1,0:T(8,128)S(1)}) fusion(f32[128]{0:T(128)S(1)} %multiply_reduce_fusion.1, bf16[128,1024]{1,0:T(8,128)(2,1)} %param.5, bf16[1920,1024]{1,0:T(8,128)(2,1)} %param.3), kind=kOutput, calls=%fused_computation.52 | convolution fusion | flops 504297600 | bytes 5185536 | tf_op jit(solution)/shard_map/dot_general | solution.py:28
  4.7 0.2 exponential_reduce_fusion.1
  4.9 0.7 broadcast_in_dim.51
  5.6 10.4 %all-to-all-start = ((f32[16,1,1920]{2,1,0:T(1,128)}), f32[16,1,1920]{2,1,0:T(1,128)S(1)}, u32[]{:S(2)}, u32[]{:S(2)}) async-start(f32[16,1,1920]{2,1,0:T(1,128)} %broadcast_in_dim.51), calls=%async_computation | async-start | bytes 245760 | tf_op jit(solution)/shard_map/all_to_all | solution.py:13
  16.7 7.9 %all-to-all-done = f32[16,1,1920]{2,1,0:T(1,128)S(1)} async-done(((f32[16,1,1920]{2,1,0:T(1,128)}), f32[16,1,1920]{2,1,0:T(1,128)S(1)}, u32[]{:S(2)}, u32[]{:S(2)}) %all-to-all-start) | async-done | bytes 122912 | tf_op jit(solution)/shard_map/all_to_all | solution.py:13
  24.6 0.1 reduce_max.37
  24.8 0.3 convert_reduce_fusion.1
  25.0 2.8 %convolution_convert_fusion.1 = bf16[128,1024]{1,0:T(8,128)(2,1)S(1)} fusion(bf16[1920,1024]{1,0:T(8,128)(2,1)} %param.3, f32[128,1920]{1,0:T(8,128)S(1)} %get-tuple-element.10, f32[1920]{0:T(1024)S(1)} %log_add_fusion.2, pred[1920]{0:T(1024)(128)(4,1)S(1)} %iota_compare_fusion), kind=kOutput, calls=%fused_computation.7 | convolution fusion | flops 504184832 | bytes 5186944 | tf_op jit(solution)/shard_map/dot_general | solution.py:39
  27.9 0.1 broadcast_select_fusion.1
  28.0 0.8 reshape.80
  28.8 10.2 %all-to-all-start.1 = ((bf16[32,4,1152]{2,1,0:T(4,128)(2,1)}), bf16[32,4,1152]{2,1,0:T(4,128)(2,1)S(1)}, u32[]{:S(2)}, u32[]{:S(2)}) async-start(bf16[32,4,1152]{2,1,0:T(4,128)(2,1)} %reshape.80), calls=%async_computation.1 | async-start | bytes 589824 | tf_op jit(solution)/shard_map/all_to_all | solution.py:47
  39.0 13.9 %all-to-all-done.1 = bf16[32,4,1152]{2,1,0:T(4,128)(2,1)S(1)} async-done(((bf16[32,4,1152]{2,1,0:T(4,128)(2,1)}), bf16[32,4,1152]{2,1,0:T(4,128)(2,1)S(1)}, u32[]{:S(2)}, u32[]{:S(2)}) %all-to-all-start.1) | async-done | bytes 294944 | tf_op jit(solution)/shard_map/all_to_all | solution.py:47
  52.8 0.1 convert_reduce_fusion.3
  53.0 0.2 fusion.15
  53.1 0.8 fusion.10
  54.0 16.8 %all_to_all.38 = bf16[32,4,1024]{2,1,0:T(4,128)(2,1)S(1)} all-to-all(bf16[32,4,1024]{2,1,0:T(4,128)(2,1)S(1)} %broadcast_in_dim.87), channel_id=1, replica_groups=mesh['items'=32,'cents'=16] {'items'}, dimensions={0} | all-to-all | bytes 524288 | tf_op jit(solution)/shard_map/all_to_all | solution.py:13
  70.8 0.2 multiply_reduce_fusion
  71.0 0.1 sub.89
  71.2 3.5 %fusion.21 = (f32[1920]{0:T(1024)S(1)}, f32[128,1920]{1,0:T(8,128)S(1)}) fusion(f32[128]{0:T(128)S(1)} %sub.89, bf16[128,1024]{1,0:T(8,128)(2,1)S(1)} %reshape.81, bf16[1920,1024]{1,0:T(8,128)(2,1)} %param.3), kind=kOutput, calls=%fused_computation.53 | convolution fusion | flops 504297600 | bytes 5185536 | tf_op jit(solution)/shard_map/dot_general | solution.py:28
  74.7 0.2 exponential_reduce_fusion
  74.9 11.2 %all_to_all.39 = f32[16,1,1920]{2,1,0:T(1,128)S(1)} all-to-all(f32[16,1,1920]{2,1,0:T(1,128)S(1)} %broadcast_in_dim.88), channel_id=1, replica_groups=mesh['items'=32,'cents'=16] {'cents'}, dimensions={0} | all-to-all | bytes 245760 | tf_op jit(solution)/shard_map/all_to_all | solution.py:13
  86.1 0.1 reduce_max.39
  86.2 0.3 convert_reduce_fusion
  86.5 2.8 %convolution_convert_fusion = bf16[128,1024]{1,0:T(8,128)(2,1)S(1)} fusion(bf16[1920,1024]{1,0:T(8,128)(2,1)} %param.3, f32[128,1920]{1,0:T(8,128)S(1)} %get-tuple-element.12, f32[1920]{0:T(1024)S(1)} %log_add_fusion, pred[1920]{0:T(1024)(128)(4,1)S(1)} %iota_compare_fusion), kind=kOutput, calls=%fused_computation.6 | convolution fusion | flops 504184832 | bytes 5186944 | tf_op jit(solution)/shard_map/dot_general | solution.py:39
  89.3 0.1 broadcast_select_fusion
  89.5 18.2 %all_to_all.40 = bf16[32,4,1152]{2,1,0:T(4,128)(2,1)S(1)} all-to-all(bf16[32,4,1152]{2,1,0:T(4,128)(2,1)S(1)} %reshape.82), channel_id=1, replica_groups=mesh['items'=32,'cents'=16] {'items'}, dimensions={0} | all-to-all | bytes 589824 | tf_op jit(solution)/shard_map/all_to_all | solution.py:47
  107.8 0.1 convert_reduce_fusion.2
  107.9 0.2 fusion.13
  108.1 0.1 fusion.11
  108.3 16.8 %all_to_all.41 = bf16[32,4,1024]{2,1,0:T(4,128)(2,1)S(1)} all-to-all(bf16[32,4,1024]{2,1,0:T(4,128)(2,1)S(1)} %broadcast_in_dim.91), channel_id=1, replica_groups=mesh['items'=32,'cents'=16] {'items'}, dimensions={0} | all-to-all | bytes 524288 | tf_op jit(solution)/shard_map/all_to_all | solution.py:13
  125.0 0.8 reshape.83
  (17 shorter events, 0.5 us)
Async XLA Ops:
  5.6 19.0 %all-to-all-start = ((f32[16,1,1920]{2,1,0:T(1,128)}), f32[16,1,1920]{2,1,0:T(1,128)S(1)}, u32[]{:S(2)}, u32[]{:S(2)}) async-start(f32[16,1,1920]{2,1,0:T(1,128)} %broadcast_in_dim.51), calls=%async_computation | async-start | bytes 245760 | tf_op jit(solution)/shard_map/all_to_all | solution.py:13
  28.8 24.0 %all-to-all-start.1 = ((bf16[32,4,1152]{2,1,0:T(4,128)(2,1)}), bf16[32,4,1152]{2,1,0:T(4,128)(2,1)S(1)}, u32[]{:S(2)}, u32[]{:S(2)}) async-start(bf16[32,4,1152]{2,1,0:T(4,128)(2,1)} %reshape.80), calls=%async_computation.1 | async-start | bytes 589824 | tf_op jit(solution)/shard_map/all_to_all | solution.py:47

commit v2 on v1

v2 whole, which is shorter than its diff:
```python
import jax
import jax.numpy as jnp
from jax import lax
from jax.experimental import pallas as pl
from jax.experimental.pallas import tpu as pltpu
from jax.sharding import PartitionSpec as P

D = 1024
ITERS = 2
CHUNK = 384
HALF = D // 2
LANES = 128
OWN = 8
WIDE = HALF + LANES
prior_count = 2.0
scale = D ** (-0.5)

f32, bf16 = jnp.float32, jnp.bfloat16
vmem = pl.BlockSpec(memory_space=pltpu.VMEM)
smem = pl.BlockSpec(memory_space=pltpu.SMEM)
hbm = pl.BlockSpec(memory_space=pltpu.HBM)


def norms_of(cents):
    wide = cents.astype(f32)
    return jnp.sum(wide * wide, axis=1, keepdims=True) * scale


def score_chunk(cents, norms, rows, start, score_ref, logs_ref):
    size = rows.shape[0]
    dots = lax.dot_general(cents, rows, (((1,), (1,)), ((), ())), preferred_element_type=f32)
    score = dots * (2.0 * scale) - norms
    score_ref[:, pl.ds(start, size)] = score
    top = jnp.max(score, axis=0, keepdims=True)
    logs = top + jnp.log(jnp.sum(jnp.exp(score - top), axis=0, keepdims=True))
    for peer in range(logs_ref.shape[0]):
        logs_ref[peer, :, pl.ds(start, size)] = logs


def first_scores(count_ref, place_ref, rows_hbm, cents_ref, rows_ref, score_ref, logs_ref, known_ref, sems):
    known_ref[0] = count_ref[0]
    known_ref[1] = place_ref[0]
    total = rows_ref.shape[0]
    copies = [
        pltpu.make_async_copy(
            rows_hbm.at[pl.ds(start, CHUNK)], rows_ref.at[pl.ds(start, CHUNK)], sems.at[i]
        )
        for i, start in enumerate(range(0, total, CHUNK))
    ]
    for copy in copies:
        copy.start()
    cents = cents_ref[...]
    norms = norms_of(cents)
    for i, start in enumerate(range(0, total, CHUNK)):
        copies[i].wait()
        score_chunk(cents, norms, rows_ref[pl.ds(start, CHUNK), :], start, score_ref, logs_ref)


def later_scores(rows_ref, blocks_ref, score_ref, logs_ref):
    total = rows_ref.shape[0]
    n_cents = blocks_ref.shape[0] // 2
    cents = jnp.concatenate([blocks_ref[:n_cents, :], blocks_ref[n_cents:, :]], axis=1)
    norms = norms_of(cents)
    for start in range(0, total, CHUNK):
        score_chunk(cents, norms, rows_ref[pl.ds(start, CHUNK), :], start, score_ref, logs_ref)


def moments(known_ref, logs_ref, score_ref, rows_ref, out_ref):
    peers, _, total = logs_ref.shape
    n_cents = score_ref.shape[0]
    high = logs_ref[0]
    for peer in range(1, peers):
        high = jnp.maximum(high, logs_ref[peer])
    mass_all = jnp.exp(logs_ref[0] - high)
    for peer in range(1, peers):
        mass_all = mass_all + jnp.exp(logs_ref[peer] - high)
    logs = high + jnp.log(mass_all)
    valid = lax.broadcasted_iota(jnp.int32, (1, total), 1) < known_ref[0]
    resp = jnp.where(valid, jnp.exp(score_ref[...] - logs), 0.0).astype(bf16)
    mass = jnp.sum(resp.astype(f32), axis=1, keepdims=True)
    moment = jnp.dot(resp, rows_ref[...], preferred_element_type=f32)
    mass_high = mass.astype(bf16)
    mass_low = (mass - mass_high.astype(f32)).astype(bf16)
    lanes = lax.broadcasted_iota(jnp.int32, (n_cents, LANES), 1)
    masses = jnp.where(lanes == 0, mass_high.astype(f32), mass_low.astype(f32)).astype(bf16)
    for half in range(2):
        out_ref[pl.ds(half * n_cents, n_cents), :HALF] = moment[
            :, half * HALF : (half + 1) * HALF
        ].astype(bf16)
        out_ref[pl.ds(half * n_cents, n_cents), HALF:] = masses


def update(parts_ref, before, out_ref):
    own = before.shape[0]
    sums = parts_ref[:own, :].astype(f32)
    for part in range(1, parts_ref.shape[0] // own):
        sums = sums + parts_ref[pl.ds(part * own, own), :].astype(f32)
    mass = sums[:, HALF : HALF + 1] + sums[:, HALF + 1 : HALF + 2]
    fresh = (sums[:, :HALF] + prior_count * before) / (mass + prior_count)
    fresh = fresh.astype(bf16)
    for part in range(out_ref.shape[0] // own):
        out_ref[pl.ds(part * own, own), :] = fresh


def first_update(known_ref, parts_ref, cents_ref, out_ref):
    n_cents = cents_ref.shape[0]
    own = OWN
    per_half = n_cents // own
    place = known_ref[1]
    row = pl.multiple_of(lax.rem(place, per_half) * own, own)
    mine = cents_ref[pl.ds(row, own), :].astype(f32)
    before = jnp.where(place < per_half, mine[:, :HALF], mine[:, HALF:])
    update(parts_ref, before, out_ref)


def later_update(parts_ref, fresh_ref, out_ref):
    update(parts_ref, fresh_ref[:OWN, :].astype(f32), out_ref)


def join(blocks_ref, out_ref):
    n_cents = out_ref.shape[0]
    for half in range(2):
        out_ref[:, half * HALF : (half + 1) * HALF] = blocks_ref[pl.ds(half * n_cents, n_cents), :]


def params(mib):
    return pltpu.CompilerParams(vmem_limit_bytes=mib << 20)


def body(embeddings, counts, centroids):
    total, n_cents = embeddings.shape[0], centroids.shape[0]
    n_items, n_split = lax.axis_size("items"), lax.axis_size("cents")
    place = lax.axis_index("items").astype(jnp.int32)[None]
    score_shape = pltpu.VMEM((n_cents, total), f32)
    logs_shape = pltpu.VMEM((n_split, 1, total), f32)
    sent_shape = pltpu.VMEM((2 * n_cents, WIDE), bf16)
    block_shape = pltpu.VMEM((2 * n_cents, HALF), bf16)

    def exchange(x, axis):
        count = lax.axis_size(axis)
        split = x.reshape(count, x.shape[0] // count, *x.shape[1:])
        return lax.all_to_all(split, axis, 0, 0).reshape(x.shape)

    rows, score, logs, known = pl.pallas_call(
        first_scores,
        out_shape=(pltpu.VMEM(embeddings.shape, bf16), score_shape, logs_shape, pltpu.SMEM((2,), jnp.int32)),
        in_specs=[smem, smem, hbm, vmem],
        out_specs=(vmem, vmem, vmem, smem),
        scratch_shapes=[pltpu.SemaphoreType.DMA((total // CHUNK,))],
        compiler_params=params(57),
        name="first_scores",
    )(counts, place, embeddings, centroids)
    fresh = blocks = None
    for step in range(ITERS):
        if step:
            score, logs = pl.pallas_call(
                later_scores,
                out_shape=(score_shape, logs_shape),
                in_specs=[vmem, vmem],
                out_specs=(vmem, vmem),
                compiler_params=params(16),
                name="later_scores",
            )(rows, blocks)
        logs = lax.all_to_all(logs, "cents", 0, 0)
        sent = pl.pallas_call(
            moments,
            out_shape=sent_shape,
            in_specs=[smem, vmem, vmem, vmem],
            out_specs=vmem,
            compiler_params=params(16),
            name="moments",
        )(known, logs, score, rows)
        parts = exchange(sent, "items")
        if step:
            fresh = pl.pallas_call(
                later_update,
                out_shape=block_shape,
                in_specs=[vmem, vmem],
                out_specs=vmem,
                compiler_params=params(16),
                name="later_update",
            )(parts, fresh)
        else:
            fresh = pl.pallas_call(
                first_update,
                out_shape=block_shape,
                in_specs=[smem, vmem, vmem],
                out_specs=vmem,
                compiler_params=params(16),
                name="first_update",
            )(known, parts, centroids)
        blocks = exchange(fresh, "items")
    return pl.pallas_call(
        join,
        out_shape=jax.ShapeDtypeStruct(centroids.shape, bf16),
        in_specs=[vmem],
        out_specs=vmem,
        compiler_params=params(16),
        name="join",
    )(blocks)


def solution(mesh):
    in_specs = (P("items", None), P("items"), P("cents", None))
    out_specs = P("cents", None)
    return jax.shard_map(body, mesh=mesh, in_specs=in_specs, out_specs=out_specs, check_vma=False)
```

time: 126 us -> 117 us (0.929)
  blocking collectives: 62.9 us -> 107 us
  waiting for transfers between devices: 21.8 us -> 0 us
  starting transfers between devices: 20.6 us -> 0 us
  matrix products: 12.8 us -> 0 us
  Pallas kernels: 0 us -> 8.54 us
  other arithmetic: 4.17 us -> 0 us
  local copies, waits for them, and re-layouts: 2.72 us -> 0.01 us
    all_to_all x4 -> x6, blocking collectives: 62.9 us -> 107 us  [the longest x4 76.9 us: exchange(): return lax.all_to_all(split, axis, 0, 0).reshape(x.shape)]
    all_to_all x2 -> x0, waiting for transfers between devices: 21.8 us -> none  [the longest x1 13.9 us: body(): parts = lax.all_to_all(sent.reshape(n_items, own, D + 128), 'items', 0, 0)]
    all_to_all x2 -> x0, starting transfers between devices: 20.6 us -> none  [the longest x1 10.4 us: gather_all(): lax.all_to_all(jnp.broadcast_to(part[None], (count,) + part.shape), axis,...]
    dot_general x4 -> x0, matrix products: 12.8 us -> none  [the longest x2 7.11 us: body(): lax.dot_general(current, embeddings, (((1,), (1,)), ((), ())), preferred_...]
    pallas_call x0 -> x7, Pallas kernels: none -> 8.54 us  [the longest x1 4.56 us: body(): pl.pallas_call(first_scores, out_shape=(pltpu.VMEM(embeddings.shape, bf16...]
    reduce_sum x10 -> x0, other arithmetic: 2.47 us -> none  [the longest x2 1.3 us: body(): norms = jnp.sum(cent_f * cent_f, axis=1)]
    reshape x4 -> x0, local copies, waits for them, and re-layouts: 1.69 us -> none  [the longest x2 0.86 us: body(): parts = lax.all_to_all(sent.reshape(n_items, own, D + 128), 'items', 0, 0)]
  transfers between devices with their start and end apart: 2 -> 0, of which waited for: 2 -> 0; matrix products, arithmetic and copies ran while one was open for 0% -> 0% of each run, Pallas kernels for 0% -> 0%
where the time goes in v2:
time: 117 us; the launch traced here: 116 us
  blocking collectives  107 us (91%)
  Pallas kernels  8.54 us (7%)
    all_to_all x4, blocking collectives, exchange(): return lax.all_to_all(split, axis, 0, 0).reshape(x.shape)  76.9 us
    all_to_all x2, blocking collectives, body(): logs = lax.all_to_all(logs, 'cents', 0, 0)  30.1 us
    pallas_call x1, Pallas kernels, body(): pl.pallas_call(first_scores, out_shape=(pltpu.VMEM(embeddings.shape, bf16...  4.56 us

profile of v2, /device:TPU:8, one launch (start us, length us, event | category | flops | bytes accessed | tf_op | source)
XLA Modules:
  0.0 116.3 jit_solution(11252837333644812468)
XLA Ops:
  0.7 4.6 %first_scores.1 = (bf16[1920,1024]{1,0:T(8,128)(2,1)S(1)}, f32[128,1920]{1,0:T(8,128)S(1)}, f32[16,1,1920]{2,1,0:T(1,128)S(1)}, s32[2]{0:T(128)S(4)}) custom-call(s32[1]{0:T(128)S(6)} %copy.4.count_ref, s32[1]{0:T(128)} %bitcast.place_ref, bf16[1920,1024]{1,0:T(8,128)(2,1)} %rows_hbm.1, bf16[128,1024]{1,0:T(8,128)(2,1)} %cents_ref.3), custom_call_target="tpu_custom_call" | custom-call | tf_op jit(solution)/shard_map/first_scores/pallas_call | solution.py:144
  5.2 0.0 copy-start
  5.2 19.0 %all_to_all.30.logs_ref = f32[16,1,1920]{2,1,0:T(1,128)S(1)} all-to-all(f32[16,1,1920]{2,1,0:T(1,128)S(1)} %get-tuple-element.13), channel_id=1, replica_groups=mesh['items'=32,'cents'=16] {'cents'}, dimensions={0} | all-to-all | bytes 245760 | tf_op jit(solution)/shard_map/all_to_all | solution.py:164
  24.2 0.8 moments.2
  25.0 24.4 %all_to_all.31 = bf16[32,8,640]{2,1,0:T(8,128)(2,1)S(1)} all-to-all(bf16[32,8,640]{2,1,0:T(8,128)(2,1)S(1)} %bitcast.11), channel_id=1, replica_groups=mesh['items'=32,'cents'=16] {'items'}, dimensions={0} | all-to-all | bytes 655360 | tf_op jit(solution)/shard_map/all_to_all | solution.py:142
  49.4 0.0 copy-done
  49.4 0.2 first_update.1.fresh_ref
  49.6 16.8 %all_to_all.32 = bf16[32,8,512]{2,1,0:T(8,128)(2,1)S(1)} all-to-all(bf16[32,8,512]{2,1,0:T(8,128)(2,1)S(1)} %bitcast.9), channel_id=1, replica_groups=mesh['items'=32,'cents'=16] {'items'}, dimensions={0} | all-to-all | bytes 524288 | tf_op jit(solution)/shard_map/all_to_all | solution.py:142
  66.4 1.3 %later_scores.1 = (f32[128,1920]{1,0:T(8,128)S(1)}, f32[16,1,1920]{2,1,0:T(1,128)S(1)}) custom-call(bf16[1920,1024]{1,0:T(8,128)(2,1)S(1)} %get-tuple-element.12.rows_ref, bf16[256,512]{1,0:T(8,128)(2,1)S(1)} %bitcast.14), custom_call_target="tpu_custom_call" | custom-call | tf_op jit(solution)/shard_map/later_scores/pallas_call | solution.py:156
  67.8 11.2 %all_to_all.33.logs_ref = f32[16,1,1920]{2,1,0:T(1,128)S(1)} all-to-all(f32[16,1,1920]{2,1,0:T(1,128)S(1)} %get-tuple-element.15), channel_id=1, replica_groups=mesh['items'=32,'cents'=16] {'cents'}, dimensions={0} | all-to-all | bytes 245760 | tf_op jit(solution)/shard_map/all_to_all | solution.py:164
  78.9 0.8 moments.3
  79.7 18.8 %all_to_all.34 = bf16[32,8,640]{2,1,0:T(8,128)(2,1)S(1)} all-to-all(bf16[32,8,640]{2,1,0:T(8,128)(2,1)S(1)} %bitcast.10), channel_id=1, replica_groups=mesh['items'=32,'cents'=16] {'items'}, dimensions={0} | all-to-all | bytes 655360 | tf_op jit(solution)/shard_map/all_to_all | solution.py:142
  98.5 0.2 later_update.1
  98.7 16.8 %all_to_all.35 = bf16[32,8,512]{2,1,0:T(8,128)(2,1)S(1)} all-to-all(bf16[32,8,512]{2,1,0:T(8,128)(2,1)S(1)} %bitcast.15), channel_id=1, replica_groups=mesh['items'=32,'cents'=16] {'items'}, dimensions={0} | all-to-all | bytes 524288 | tf_op jit(solution)/shard_map/all_to_all | solution.py:142
  115.5 0.7 join.1
Async XLA Ops:
  5.2 44.2 %copy-start = (bf16[128,1024]{1,0:T(8,128)(2,1)S(1)}, bf16[128,1024]{1,0:T(8,128)(2,1)}, u32[]{:S(2)}) copy-start(bf16[128,1024]{1,0:T(8,128)(2,1)} %cents_ref.3) | copy-start | bytes 786436

commit v3 on v2

--- a/solution.py
+++ b/solution.py
@@ -8,10 +8,9 @@
 D = 1024
 ITERS = 2
 CHUNK = 384
-HALF = D // 2
 LANES = 128
-OWN = 8
-WIDE = HALF + LANES
+TILE = 8
+WIDE = D + LANES
 prior_count = 2.0
 scale = D ** (-0.5)
 
@@ -37,29 +36,39 @@
         logs_ref[peer, :, pl.ds(start, size)] = logs
 
 
-def first_scores(count_ref, place_ref, rows_hbm, cents_ref, rows_ref, score_ref, logs_ref, known_ref, sems):
-    known_ref[0] = count_ref[0]
-    known_ref[1] = place_ref[0]
+def first_scores(
+    count_ref, place_ref, rows_hbm, cents_hbm, rows_ref, score_ref, logs_ref, known_ref, cents_ref, sems
+):
     total = rows_ref.shape[0]
+    starts = range(0, total, CHUNK)
+    cents_copy = pltpu.make_async_copy(cents_hbm, cents_ref, sems.at[len(starts)])
+    cents_copy.start()
     copies = [
         pltpu.make_async_copy(
             rows_hbm.at[pl.ds(start, CHUNK)], rows_ref.at[pl.ds(start, CHUNK)], sems.at[i]
         )
-        for i, start in enumerate(range(0, total, CHUNK))
+        for i, start in enumerate(starts)
     ]
     for copy in copies:
         copy.start()
+    known_ref[0] = count_ref[0]
+    known_ref[1] = place_ref[0]
+    cents_copy.wait()
     cents = cents_ref[...]
     norms = norms_of(cents)
-    for i, start in enumerate(range(0, total, CHUNK)):
-        copies[i].wait()
+    for copy, start in zip(copies, starts):
+        copy.wait()
         score_chunk(cents, norms, rows_ref[pl.ds(start, CHUNK), :], start, score_ref, logs_ref)
+
+
+def flat(blocks_ref):
+    parts, own, width = blocks_ref.shape
+    return blocks_ref[...].reshape(parts * own, width)
 
 
 def later_scores(rows_ref, blocks_ref, score_ref, logs_ref):
     total = rows_ref.shape[0]
-    n_cents = blocks_ref.shape[0] // 2
-    cents = jnp.concatenate([blocks_ref[:n_cents, :], blocks_ref[n_cents:, :]], axis=1)
+    cents = flat(blocks_ref)
     norms = norms_of(cents)
     for start in range(0, total, CHUNK):
         score_chunk(cents, norms, rows_ref[pl.ds(start, CHUNK), :], start, score_ref, logs_ref)
@@ -83,44 +92,38 @@
     mass_low = (mass - mass_high.astype(f32)).astype(bf16)
     lanes = lax.broadcasted_iota(jnp.int32, (n_cents, LANES), 1)
     masses = jnp.where(lanes == 0, mass_high.astype(f32), mass_low.astype(f32)).astype(bf16)
-    for half in range(2):
-        out_ref[pl.ds(half * n_cents, n_cents), :HALF] = moment[
-            :, half * HALF : (half + 1) * HALF
-        ].astype(bf16)
-        out_ref[pl.ds(half * n_cents, n_cents), HALF:] = masses
+    parts, own, _ = out_ref.shape
+    out_ref[:, :, :D] = moment.astype(bf16).reshape(parts, own, D)
+    out_ref[:, :, D:] = masses.reshape(parts, own, LANES)
 
 
 def update(parts_ref, before, out_ref):
-    own = before.shape[0]
-    sums = parts_ref[:own, :].astype(f32)
-    for part in range(1, parts_ref.shape[0] // own):
-        sums = sums + parts_ref[pl.ds(part * own, own), :].astype(f32)
-    mass = sums[:, HALF : HALF + 1] + sums[:, HALF + 1 : HALF + 2]
-    fresh = (sums[:, :HALF] + prior_count * before) / (mass + prior_count)
-    fresh = fresh.astype(bf16)
-    for part in range(out_ref.shape[0] // own):
-        out_ref[pl.ds(part * own, own), :] = fresh
+    sums = parts_ref[0].astype(f32)
+    for part in range(1, parts_ref.shape[0]):
+        sums = sums + parts_ref[part].astype(f32)
+    mass = sums[:, D : D + 1] + sums[:, D + 1 : D + 2]
+    fresh = ((sums[:, :D] + prior_count * before) / (mass + prior_count)).astype(bf16)
+    for part in range(out_ref.shape[0]):
+        out_ref[part] = fresh
 
 
 def first_update(known_ref, parts_ref, cents_ref, out_ref):
-    n_cents = cents_ref.shape[0]
-    own = OWN
-    per_half = n_cents // own
+    own = out_ref.shape[1]
     place = known_ref[1]
-    row = pl.multiple_of(lax.rem(place, per_half) * own, own)
-    mine = cents_ref[pl.ds(row, own), :].astype(f32)
-    before = jnp.where(place < per_half, mine[:, :HALF], mine[:, HALF:])
+    row = pl.multiple_of(place * own // TILE * TILE, TILE)
+    near = cents_ref[pl.ds(row, TILE), :].astype(f32)
+    before = near[:own]
+    for skip in range(own, TILE, own):
+        before = jnp.where(place * own == row + skip, near[skip : skip + own], before)
     update(parts_ref, before, out_ref)
 
 
 def later_update(parts_ref, fresh_ref, out_ref):
-    update(parts_ref, fresh_ref[:OWN, :].astype(f32), out_ref)
+    update(parts_ref, fresh_ref[0].astype(f32), out_ref)
 
 
 def join(blocks_ref, out_ref):
-    n_cents = out_ref.shape[0]
-    for half in range(2):
-        out_ref[:, half * HALF : (half + 1) * HALF] = blocks_ref[pl.ds(half * n_cents, n_cents), :]
+    out_ref[...] = flat(blocks_ref)
 
 
 def params(mib):
@@ -133,20 +136,18 @@
     place = lax.axis_index("items").astype(jnp.int32)[None]
     score_shape = pltpu.VMEM((n_cents, total), f32)
     logs_shape = pltpu.VMEM((n_split, 1, total), f32)
-    sent_shape = pltpu.VMEM((2 * n_cents, WIDE), bf16)
-    block_shape = pltpu.VMEM((2 * n_cents, HALF), bf16)
-
-    def exchange(x, axis):
-        count = lax.axis_size(axis)
-        split = x.reshape(count, x.shape[0] // count, *x.shape[1:])
-        return lax.all_to_all(split, axis, 0, 0).reshape(x.shape)
+    sent_shape = pltpu.VMEM((n_items, n_cents // n_items, WIDE), bf16)
+    block_shape = pltpu.VMEM((n_items, n_cents // n_items, D), bf16)
 
     rows, score, logs, known = pl.pallas_call(
         first_scores,
         out_shape=(pltpu.VMEM(embeddings.shape, bf16), score_shape, logs_shape, pltpu.SMEM((2,), jnp.int32)),
-        in_specs=[smem, smem, hbm, vmem],
+        in_specs=[smem, smem, hbm, hbm],
         out_specs=(vmem, vmem, vmem, smem),
-        scratch_shapes=[pltpu.SemaphoreType.DMA((total // CHUNK,))],
+        scratch_shapes=[
+            pltpu.VMEM(centroids.shape, bf16),
+            pltpu.SemaphoreType.DMA((total // CHUNK + 1,)),
+        ],
         compiler_params=params(57),
         name="first_scores",
     )(counts, place, embeddings, centroids)
@@ -170,7 +171,7 @@
             compiler_params=params(16),
             name="moments",
         )(known, logs, score, rows)
-        parts = exchange(sent, "items")
+        parts = lax.all_to_all(sent, "items", 0, 0)
         if step:
             fresh = pl.pallas_call(
                 later_update,
@@ -189,7 +190,7 @@
                 compiler_params=params(16),
                 name="first_update",
             )(known, parts, centroids)
-        blocks = exchange(fresh, "items")
+        blocks = lax.all_to_all(fresh, "items", 0, 0)
     return pl.pallas_call(
         join,
         out_shape=jax.ShapeDtypeStruct(centroids.shape, bf16),

time: 117 us -> 114 us (0.974)
    all_to_all x4, blocking collectives: 76.9 us -> 75.5 us  [the longest x2 42 us: body(): parts = lax.all_to_all(sent, 'items', 0, 0)]
where the time goes in v3:
time: 114 us
  blocking collectives  106 us (93%)
  Pallas kernels  7.73 us (7%)
    all_to_all x2, blocking collectives, body(): parts = lax.all_to_all(sent, 'items', 0, 0)  42 us
    all_to_all x2, blocking collectives, body(): blocks = lax.all_to_all(fresh, 'items', 0, 0)  33.5 us
    all_to_all x2, blocking collectives, body(): logs = lax.all_to_all(logs, 'cents', 0, 0)  30.1 us
    pallas_call x1, Pallas kernels, body(): pl.pallas_call(first_scores, out_shape=(pltpu.VMEM(embeddings.shape, bf16...  3.7 us

profile of v3, /device:TPU:8, one launch (start us, length us, event | category | flops | bytes accessed | tf_op | source)
XLA Modules:
  0.0 114.1 jit_solution(18413693736949100547)
XLA Ops:
  0.7 3.7 %first_scores.1 = (bf16[1920,1024]{1,0:T(8,128)(2,1)S(1)}, f32[128,1920]{1,0:T(8,128)S(1)}, f32[16,1,1920]{2,1,0:T(1,128)S(1)}, s32[2]{0:T(128)S(4)}) custom-call(s32[1]{0:T(128)S(6)} %copy.4.count_ref, s32[1]{0:T(128)} %bitcast.place_ref, bf16[1920,1024]{1,0:T(8,128)(2,1)} %rows_hbm.1, bf16[128,1024]{1,0:T(8,128)(2,1)} %cents_ref.1), custom_call_target="tpu_custom_call" | custom-call | tf_op jit(solution)/shard_map/first_scores/pallas_call | solution.py:142
  4.4 0.0 copy-start
  4.4 19.0 %all_to_all.30.logs_ref = f32[16,1,1920]{2,1,0:T(1,128)S(1)} all-to-all(f32[16,1,1920]{2,1,0:T(1,128)S(1)} %get-tuple-element.13), channel_id=1, replica_groups=mesh['items'=32,'cents'=16] {'cents'}, dimensions={0} | all-to-all | bytes 245760 | tf_op jit(solution)/shard_map/all_to_all | solution.py:165
  23.3 0.8 moments.2
  24.1 23.8 %all_to_all.31.parts_ref = bf16[32,4,1152]{2,1,0:T(4,128)(2,1)S(1)} all-to-all(bf16[32,4,1152]{2,1,0:T(4,128)(2,1)S(1)} %moments.2), channel_id=1, replica_groups=mesh['items'=32,'cents'=16] {'items'}, dimensions={0} | all-to-all | bytes 589824 | tf_op jit(solution)/shard_map/all_to_all | solution.py:174
  47.9 0.0 copy-done
  47.9 0.2 first_update.1.fresh_ref
  48.1 16.8 %all_to_all.32.blocks_ref = bf16[32,4,1024]{2,1,0:T(4,128)(2,1)S(1)} all-to-all(bf16[32,4,1024]{2,1,0:T(4,128)(2,1)S(1)} %first_update.1.fresh_ref), channel_id=1, replica_groups=mesh['items'=32,'cents'=16] {'items'}, dimensions={0} | all-to-all | bytes 524288 | tf_op jit(solution)/shard_map/all_to_all | solution.py:193
  64.9 1.4 %later_scores.1 = (f32[128,1920]{1,0:T(8,128)S(1)}, f32[16,1,1920]{2,1,0:T(1,128)S(1)}) custom-call(bf16[1920,1024]{1,0:T(8,128)(2,1)S(1)} %get-tuple-element.12.rows_ref, bf16[32,4,1024]{2,1,0:T(4,128)(2,1)S(1)} %all_to_all.32.blocks_ref), custom_call_target="tpu_custom_call" | custom-call | tf_op jit(solution)/shard_map/later_scores/pallas_call | solution.py:157
  66.3 11.2 %all_to_all.33.logs_ref = f32[16,1,1920]{2,1,0:T(1,128)S(1)} all-to-all(f32[16,1,1920]{2,1,0:T(1,128)S(1)} %get-tuple-element.15), channel_id=1, replica_groups=mesh['items'=32,'cents'=16] {'cents'}, dimensions={0} | all-to-all | bytes 245760 | tf_op jit(solution)/shard_map/all_to_all | solution.py:165
  77.4 0.8 moments.3
  78.2 18.2 %all_to_all.34.parts_ref = bf16[32,4,1152]{2,1,0:T(4,128)(2,1)S(1)} all-to-all(bf16[32,4,1152]{2,1,0:T(4,128)(2,1)S(1)} %moments.3), channel_id=1, replica_groups=mesh['items'=32,'cents'=16] {'items'}, dimensions={0} | all-to-all | bytes 589824 | tf_op jit(solution)/shard_map/all_to_all | solution.py:174
  96.4 0.2 later_update.1
  96.6 16.8 %all_to_all.35.blocks_ref = bf16[32,4,1024]{2,1,0:T(4,128)(2,1)S(1)} all-to-all(bf16[32,4,1024]{2,1,0:T(4,128)(2,1)S(1)} %later_update.1), channel_id=1, replica_groups=mesh['items'=32,'cents'=16] {'items'}, dimensions={0} | all-to-all | bytes 524288 | tf_op jit(solution)/shard_map/all_to_all | solution.py:193
  113.4 0.7 join.1
Async XLA Ops:
  4.4 43.6 %copy-start = (bf16[128,1024]{1,0:T(8,128)(2,1)S(1)}, bf16[128,1024]{1,0:T(8,128)(2,1)}, u32[]{:S(2)}) copy-start(bf16[128,1024]{1,0:T(8,128)(2,1)} %cents_ref.1) | copy-start | bytes 786436

commit v4 on v3

--- a/solution.py
+++ b/solution.py
@@ -7,7 +7,9 @@
 
 D = 1024
 ITERS = 2
-CHUNK = 384
+CHUNK = 128
+PIECE = 384
+EARLY = 2
 LANES = 128
 TILE = 8
 WIDE = D + LANES
@@ -25,27 +27,36 @@
     return jnp.sum(wide * wide, axis=1, keepdims=True) * scale
 
 
-def score_chunk(cents, norms, rows, start, score_ref, logs_ref):
-    size = rows.shape[0]
+def dot_chunk(cents, norms, rows_ref, start, size, score_ref):
+    rows = rows_ref[pl.ds(start, size), :]
     dots = lax.dot_general(cents, rows, (((1,), (1,)), ((), ())), preferred_element_type=f32)
-    score = dots * (2.0 * scale) - norms
-    score_ref[:, pl.ds(start, size)] = score
+    score_ref[:, pl.ds(start, size)] = dots * (2.0 * scale) - norms
+
+
+def logs_chunk(score_ref, start, size, logs_ref):
+    score = score_ref[:, pl.ds(start, size)]
     top = jnp.max(score, axis=0, keepdims=True)
     logs = top + jnp.log(jnp.sum(jnp.exp(score - top), axis=0, keepdims=True))
     for peer in range(logs_ref.shape[0]):
         logs_ref[peer, :, pl.ds(start, size)] = logs
 
 
+def score_span(cents, norms, rows_ref, first, last, score_ref, logs_ref):
+    for start in range(first, last, CHUNK):
+        dot_chunk(cents, norms, rows_ref, start, CHUNK, score_ref)
+        logs_chunk(score_ref, start, CHUNK, logs_ref)
+
+
 def first_scores(
     count_ref, place_ref, rows_hbm, cents_hbm, rows_ref, score_ref, logs_ref, known_ref, cents_ref, sems
 ):
     total = rows_ref.shape[0]
-    starts = range(0, total, CHUNK)
+    starts = range(0, total, PIECE)
     cents_copy = pltpu.make_async_copy(cents_hbm, cents_ref, sems.at[len(starts)])
     cents_copy.start()
     copies = [
         pltpu.make_async_copy(
-            rows_hbm.at[pl.ds(start, CHUNK)], rows_ref.at[pl.ds(start, CHUNK)], sems.at[i]
+            rows_hbm.at[pl.ds(start, PIECE)], rows_ref.at[pl.ds(start, PIECE)], sems.at[i]
         )
         for i, start in enumerate(starts)
     ]
@@ -56,9 +67,12 @@
     cents_copy.wait()
     cents = cents_ref[...]
     norms = norms_of(cents)
-    for copy, start in zip(copies, starts):
+    for copy in copies[:EARLY]:
         copy.wait()
-        score_chunk(cents, norms, rows_ref[pl.ds(start, CHUNK), :], start, score_ref, logs_ref)
+    score_span(cents, norms, rows_ref, 0, EARLY * PIECE, score_ref, logs_ref)
+    for copy in copies[EARLY:]:
+        copy.wait()
+    score_span(cents, norms, rows_ref, EARLY * PIECE, total, score_ref, logs_ref)
 
 
 def flat(blocks_ref):
@@ -67,11 +81,8 @@
 
 
 def later_scores(rows_ref, blocks_ref, score_ref, logs_ref):
-    total = rows_ref.shape[0]
     cents = flat(blocks_ref)
-    norms = norms_of(cents)
-    for start in range(0, total, CHUNK):
-        score_chunk(cents, norms, rows_ref[pl.ds(start, CHUNK), :], start, score_ref, logs_ref)
+    score_span(cents, norms_of(cents), rows_ref, 0, rows_ref.shape[0], score_ref, logs_ref)
 
 
 def moments(known_ref, logs_ref, score_ref, rows_ref, out_ref):
@@ -146,7 +157,7 @@
         out_specs=(vmem, vmem, vmem, smem),
         scratch_shapes=[
             pltpu.VMEM(centroids.shape, bf16),
-            pltpu.SemaphoreType.DMA((total // CHUNK + 1,)),
+            pltpu.SemaphoreType.DMA((total // PIECE + 1,)),
         ],
         compiler_params=params(57),
         name="first_scores",

time: 114 us -> 114 us (level)
  no operation moved by 1% of the time
where the time goes in v4:
time: 114 us; the launch traced here: 113 us
  blocking collectives  106 us (93%)
  Pallas kernels  7.07 us (6%)
    all_to_all x2, blocking collectives, body(): parts = lax.all_to_all(sent, 'items', 0, 0)  42 us
    all_to_all x2, blocking collectives, body(): blocks = lax.all_to_all(fresh, 'items', 0, 0)  33.5 us
    all_to_all x2, blocking collectives, body(): logs = lax.all_to_all(logs, 'cents', 0, 0)  30.1 us
    pallas_call x1, Pallas kernels, body(): pl.pallas_call(first_scores, out_shape=(pltpu.VMEM(embeddings.shape, bf16...  3.12 us

profile of v4, /device:TPU:8, one launch (start us, length us, event | category | flops | bytes accessed | tf_op | source)
XLA Modules:
  0.0 113.4 jit_solution(8830682958902097168)
XLA Ops:
  0.7 3.1 %first_scores.1 = (bf16[1920,1024]{1,0:T(8,128)(2,1)S(1)}, f32[128,1920]{1,0:T(8,128)S(1)}, f32[16,1,1920]{2,1,0:T(1,128)S(1)}, s32[2]{0:T(128)S(4)}) custom-call(s32[1]{0:T(128)S(6)} %copy.4.count_ref, s32[1]{0:T(128)} %bitcast.place_ref, bf16[1920,1024]{1,0:T(8,128)(2,1)} %rows_hbm.1, bf16[128,1024]{1,0:T(8,128)(2,1)} %cents_ref.1), custom_call_target="tpu_custom_call" | custom-call | tf_op jit(solution)/shard_map/first_scores/pallas_call | solution.py:153
  3.8 0.0 copy-start
  3.8 19.0 %all_to_all.30.logs_ref = f32[16,1,1920]{2,1,0:T(1,128)S(1)} all-to-all(f32[16,1,1920]{2,1,0:T(1,128)S(1)} %get-tuple-element.13), channel_id=1, replica_groups=mesh['items'=32,'cents'=16] {'cents'}, dimensions={0} | all-to-all | bytes 245760 | tf_op jit(solution)/shard_map/all_to_all | solution.py:176
  22.7 0.8 moments.2
  23.5 23.8 %all_to_all.31.parts_ref = bf16[32,4,1152]{2,1,0:T(4,128)(2,1)S(1)} all-to-all(bf16[32,4,1152]{2,1,0:T(4,128)(2,1)S(1)} %moments.2), channel_id=1, replica_groups=mesh['items'=32,'cents'=16] {'items'}, dimensions={0} | all-to-all | bytes 589824 | tf_op jit(solution)/shard_map/all_to_all | solution.py:185
  47.3 0.0 copy-done
  47.4 0.2 first_update.1.fresh_ref
  47.6 16.8 %all_to_all.32.blocks_ref = bf16[32,4,1024]{2,1,0:T(4,128)(2,1)S(1)} all-to-all(bf16[32,4,1024]{2,1,0:T(4,128)(2,1)S(1)} %first_update.1.fresh_ref), channel_id=1, replica_groups=mesh['items'=32,'cents'=16] {'items'}, dimensions={0} | all-to-all | bytes 524288 | tf_op jit(solution)/shard_map/all_to_all | solution.py:204
  64.3 1.3 %later_scores.1 = (f32[128,1920]{1,0:T(8,128)S(1)}, f32[16,1,1920]{2,1,0:T(1,128)S(1)}) custom-call(bf16[1920,1024]{1,0:T(8,128)(2,1)S(1)} %get-tuple-element.12.rows_ref, bf16[32,4,1024]{2,1,0:T(4,128)(2,1)S(1)} %all_to_all.32.blocks_ref), custom_call_target="tpu_custom_call" | custom-call | tf_op jit(solution)/shard_map/later_scores/pallas_call | solution.py:168
  65.6 11.2 %all_to_all.33.logs_ref = f32[16,1,1920]{2,1,0:T(1,128)S(1)} all-to-all(f32[16,1,1920]{2,1,0:T(1,128)S(1)} %get-tuple-element.15), channel_id=1, replica_groups=mesh['items'=32,'cents'=16] {'cents'}, dimensions={0} | all-to-all | bytes 245760 | tf_op jit(solution)/shard_map/all_to_all | solution.py:176
  76.8 0.8 moments.3
  77.5 18.2 %all_to_all.34.parts_ref = bf16[32,4,1152]{2,1,0:T(4,128)(2,1)S(1)} all-to-all(bf16[32,4,1152]{2,1,0:T(4,128)(2,1)S(1)} %moments.3), channel_id=1, replica_groups=mesh['items'=32,'cents'=16] {'items'}, dimensions={0} | all-to-all | bytes 589824 | tf_op jit(solution)/shard_map/all_to_all | solution.py:185
  95.7 0.2 later_update.1
  96.0 16.8 %all_to_all.35.blocks_ref = bf16[32,4,1024]{2,1,0:T(4,128)(2,1)S(1)} all-to-all(bf16[32,4,1024]{2,1,0:T(4,128)(2,1)S(1)} %later_update.1), channel_id=1, replica_groups=mesh['items'=32,'cents'=16] {'items'}, dimensions={0} | all-to-all | bytes 524288 | tf_op jit(solution)/shard_map/all_to_all | solution.py:204
  112.7 0.7 join.1
Async XLA Ops:
  3.8 43.6 %copy-start = (bf16[128,1024]{1,0:T(8,128)(2,1)S(1)}, bf16[128,1024]{1,0:T(8,128)(2,1)}, u32[]{:S(2)}) copy-start(bf16[128,1024]{1,0:T(8,128)(2,1)} %cents_ref.1) | copy-start | bytes 786436

commit v5 on v4

--- a/solution.py
+++ b/solution.py
@@ -12,7 +12,8 @@
 EARLY = 2
 LANES = 128
 TILE = 8
-WIDE = D + LANES
+HALF = D // 2
+SUB = 4
 prior_count = 2.0
 scale = D ** (-0.5)
 
@@ -75,13 +76,8 @@
     score_span(cents, norms, rows_ref, EARLY * PIECE, total, score_ref, logs_ref)
 
 
-def flat(blocks_ref):
-    parts, own, width = blocks_ref.shape
-    return blocks_ref[...].reshape(parts * own, width)
-
-
-def later_scores(rows_ref, blocks_ref, score_ref, logs_ref):
-    cents = flat(blocks_ref)
+def later_scores(rows_ref, cents_ref, score_ref, logs_ref):
+    cents = cents_ref[...]
     score_span(cents, norms_of(cents), rows_ref, 0, rows_ref.shape[0], score_ref, logs_ref)
 
 
@@ -99,42 +95,49 @@
     resp = jnp.where(valid, jnp.exp(score_ref[...] - logs), 0.0).astype(bf16)
     mass = jnp.sum(resp.astype(f32), axis=1, keepdims=True)
     moment = jnp.dot(resp, rows_ref[...], preferred_element_type=f32)
-    mass_high = mass.astype(bf16)
-    mass_low = (mass - mass_high.astype(f32)).astype(bf16)
+    groups, halves = out_ref.shape[:2]
+    pieces = HALF // LANES
+    for half in range(halves):
+        for piece in range(pieces):
+            start = half * HALF + piece * LANES
+            tile = moment[:, start : start + LANES].astype(bf16).reshape(groups, 2, SUB, LANES)
+            for low in range(2):
+                out_ref[:, half, low * pieces + piece] = tile[:, low]
+    mass_high = mass.astype(bf16).astype(f32)
     lanes = lax.broadcasted_iota(jnp.int32, (n_cents, LANES), 1)
-    masses = jnp.where(lanes == 0, mass_high.astype(f32), mass_low.astype(f32)).astype(bf16)
-    parts, own, _ = out_ref.shape
-    out_ref[:, :, :D] = moment.astype(bf16).reshape(parts, own, D)
-    out_ref[:, :, D:] = masses.reshape(parts, own, LANES)
+    masses = jnp.where(lanes % 2 == 0, mass_high, mass - mass_high).reshape(groups, 2, SUB, LANES)
+    lanes = lax.broadcasted_iota(jnp.int32, (groups, SUB, LANES), 2)
+    tile = jnp.where(lanes < 2, masses[:, 0], masses[:, 1]).astype(bf16)
+    for half in range(halves):
+        out_ref[:, half, 2 * pieces] = tile
 
 
 def update(parts_ref, before, out_ref):
     sums = parts_ref[0].astype(f32)
     for part in range(1, parts_ref.shape[0]):
         sums = sums + parts_ref[part].astype(f32)
-    mass = sums[:, D : D + 1] + sums[:, D + 1 : D + 2]
-    fresh = ((sums[:, :D] + prior_count * before) / (mass + prior_count)).astype(bf16)
+    pieces = HALF // LANES
+    masses = sums[2 * pieces]
+    rows = []
+    for low in range(2):
+        mass = masses[:, 2 * low : 2 * low + 1] + masses[:, 2 * low + 1 : 2 * low + 2]
+        moment = jnp.concatenate([sums[low * pieces + piece] for piece in range(pieces)], axis=1)
+        old = before[low * SUB : (low + 1) * SUB]
+        rows.append((moment + prior_count * old) / (mass + prior_count))
+    fresh = jnp.concatenate(rows, axis=0).astype(bf16)
     for part in range(out_ref.shape[0]):
         out_ref[part] = fresh
 
 
 def first_update(known_ref, parts_ref, cents_ref, out_ref):
-    own = out_ref.shape[1]
     place = known_ref[1]
-    row = pl.multiple_of(place * own // TILE * TILE, TILE)
+    row = pl.multiple_of(place // 2 * TILE, TILE)
     near = cents_ref[pl.ds(row, TILE), :].astype(f32)
-    before = near[:own]
-    for skip in range(own, TILE, own):
-        before = jnp.where(place * own == row + skip, near[skip : skip + own], before)
-    update(parts_ref, before, out_ref)
+    update(parts_ref, jnp.where(place % 2 == 0, near[:, :HALF], near[:, HALF:]), out_ref)
 
 
 def later_update(parts_ref, fresh_ref, out_ref):
     update(parts_ref, fresh_ref[0].astype(f32), out_ref)
-
-
-def join(blocks_ref, out_ref):
-    out_ref[...] = flat(blocks_ref)
 
 
 def params(mib):
@@ -147,8 +150,8 @@
     place = lax.axis_index("items").astype(jnp.int32)[None]
     score_shape = pltpu.VMEM((n_cents, total), f32)
     logs_shape = pltpu.VMEM((n_split, 1, total), f32)
-    sent_shape = pltpu.VMEM((n_items, n_cents // n_items, WIDE), bf16)
-    block_shape = pltpu.VMEM((n_items, n_cents // n_items, D), bf16)
+    sent_shape = pltpu.VMEM((n_cents // TILE, 2, 2 * HALF // LANES + 1, SUB, LANES), bf16)
+    block_shape = pltpu.VMEM((n_items, TILE, HALF), bf16)
 
     rows, score, logs, known = pl.pallas_call(
         first_scores,
@@ -162,7 +165,7 @@
         compiler_params=params(57),
         name="first_scores",
     )(counts, place, embeddings, centroids)
-    fresh = blocks = None
+    fresh = current = None
     for step in range(ITERS):
         if step:
             score, logs = pl.pallas_call(
@@ -172,7 +175,7 @@
                 out_specs=(vmem, vmem),
                 compiler_params=params(16),
                 name="later_scores",
-            )(rows, blocks)
+            )(rows, current)
         logs = lax.all_to_all(logs, "cents", 0, 0)
         sent = pl.pallas_call(
             moments,
@@ -182,7 +185,7 @@
             compiler_params=params(16),
             name="moments",
         )(known, logs, score, rows)
-        parts = lax.all_to_all(sent, "items", 0, 0)
+        parts = lax.all_to_all(sent.reshape(n_items, *sent.shape[2:]), "items", 0, 0)
         if step:
             fresh = pl.pallas_call(
                 later_update,
@@ -202,14 +205,9 @@
                 name="first_update",
             )(known, parts, centroids)
         blocks = lax.all_to_all(fresh, "items", 0, 0)
-    return pl.pallas_call(
-        join,
-        out_shape=jax.ShapeDtypeStruct(centroids.shape, bf16),
-        in_specs=[vmem],
-        out_specs=vmem,
-        compiler_params=params(16),
-        name="join",
-    )(blocks)
+        blocks = blocks.reshape(n_cents // TILE, 2, TILE, HALF).transpose(0, 2, 1, 3)
+        current = blocks.reshape(n_cents, D)
+    return current
 
 
 def solution(mesh):

time: 114 us -> 114 us (level)
  no operation moved by 1% of the time
where the time goes in v5:
time: 114 us; the launch traced here: 113 us
  blocking collectives  106 us (93%)
  Pallas kernels  6.36 us (6%)
    all_to_all x2, blocking collectives, body(): lax.all_to_all(sent.reshape(n_items, *sent.shape[2:]), 'items', 0, 0)  42 us
    all_to_all x2, blocking collectives, body(): blocks = lax.all_to_all(fresh, 'items', 0, 0)  33.5 us
    all_to_all x2, blocking collectives, body(): logs = lax.all_to_all(logs, 'cents', 0, 0)  30.1 us
    pallas_call x1, Pallas kernels, body(): pl.pallas_call(first_scores, out_shape=(pltpu.VMEM(embeddings.shape, bf16...  3.12 us

profile of v5, /device:TPU:8, one launch (start us, length us, event | category | flops | bytes accessed | tf_op | source)
XLA Modules:
  0.0 113.4 jit_solution(5791437417105006071)
XLA Ops:
  0.7 3.1 %first_scores.1 = (bf16[1920,1024]{1,0:T(8,128)(2,1)S(1)}, f32[128,1920]{1,0:T(8,128)S(1)}, f32[16,1,1920]{2,1,0:T(1,128)S(1)}, s32[2]{0:T(128)S(4)}) custom-call(s32[1]{0:T(128)S(6)} %copy.5.count_ref, s32[1]{0:T(128)} %bitcast.place_ref, bf16[1920,1024]{1,0:T(8,128)(2,1)} %rows_hbm.1, bf16[128,1024]{1,0:T(8,128)(2,1)} %cents_ref.1), custom_call_target="tpu_custom_call" | custom-call | tf_op jit(solution)/shard_map/first_scores/pallas_call | solution.py:156
  3.8 0.0 copy-start
  3.8 19.0 %all_to_all.30.logs_ref = f32[16,1,1920]{2,1,0:T(1,128)S(1)} all-to-all(f32[16,1,1920]{2,1,0:T(1,128)S(1)} %get-tuple-element.13), channel_id=1, replica_groups=mesh['items'=32,'cents'=16] {'cents'}, dimensions={0} | all-to-all | bytes 245760 | tf_op jit(solution)/shard_map/all_to_all | solution.py:179
  22.7 0.8 moments.2
  23.5 23.8 %all_to_all.31.parts_ref = bf16[32,9,4,128]{3,2,1,0:T(4,128)(2,1)S(1)} all-to-all(bf16[32,9,4,128]{3,2,1,0:T(4,128)(2,1)S(1)} %bitcast.14), channel_id=1, replica_groups=mesh['items'=32,'cents'=16] {'items'}, dimensions={0} | all-to-all | bytes 589824 | tf_op jit(solution)/shard_map/all_to_all | solution.py:188
  47.4 0.0 copy-done
  47.4 0.2 first_update.1.fresh_ref
  47.6 16.8 %all_to_all.32 = bf16[32,8,512]{2,1,0:T(8,128)(2,1)S(1)} all-to-all(bf16[32,8,512]{2,1,0:T(8,128)(2,1)S(1)} %first_update.1.fresh_ref), channel_id=1, replica_groups=mesh['items'=32,'cents'=16] {'items'}, dimensions={0} | all-to-all | bytes 524288 | tf_op jit(solution)/shard_map/all_to_all | solution.py:207
  64.3 1.3 %later_scores.1 = (f32[128,1920]{1,0:T(8,128)S(1)}, f32[16,1,1920]{2,1,0:T(1,128)S(1)}) custom-call(bf16[1920,1024]{1,0:T(8,128)(2,1)S(1)} %get-tuple-element.12.rows_ref, bf16[128,1024]{1,0:T(8,128)(2,1)S(1)} %bitcast.15), custom_call_target="tpu_custom_call" | custom-call | tf_op jit(solution)/shard_map/later_scores/pallas_call | solution.py:171
  65.6 11.2 %all_to_all.33.logs_ref = f32[16,1,1920]{2,1,0:T(1,128)S(1)} all-to-all(f32[16,1,1920]{2,1,0:T(1,128)S(1)} %get-tuple-element.15), channel_id=1, replica_groups=mesh['items'=32,'cents'=16] {'cents'}, dimensions={0} | all-to-all | bytes 245760 | tf_op jit(solution)/shard_map/all_to_all | solution.py:179
  76.8 0.8 moments.3
  77.6 18.2 %all_to_all.34.parts_ref = bf16[32,9,4,128]{3,2,1,0:T(4,128)(2,1)S(1)} all-to-all(bf16[32,9,4,128]{3,2,1,0:T(4,128)(2,1)S(1)} %bitcast.13), channel_id=1, replica_groups=mesh['items'=32,'cents'=16] {'items'}, dimensions={0} | all-to-all | bytes 589824 | tf_op jit(solution)/shard_map/all_to_all | solution.py:188
  95.8 0.2 later_update.1
  96.0 16.8 %all_to_all.35 = bf16[32,8,512]{2,1,0:T(8,128)(2,1)S(1)} all-to-all(bf16[32,8,512]{2,1,0:T(8,128)(2,1)S(1)} %later_update.1), channel_id=1, replica_groups=mesh['items'=32,'cents'=16] {'items'}, dimensions={0} | all-to-all | bytes 524288 | tf_op jit(solution)/shard_map/all_to_all | solution.py:207
  112.7 0.7 copy.6
Async XLA Ops:
  3.8 43.6 %copy-start = (bf16[128,1024]{1,0:T(8,128)(2,1)S(1)}, bf16[128,1024]{1,0:T(8,128)(2,1)}, u32[]{:S(2)}) copy-start(bf16[128,1024]{1,0:T(8,128)(2,1)} %cents_ref.1) | copy-start | bytes 786436

commit v6 on v5

--- a/solution.py
+++ b/solution.py
@@ -15,6 +15,8 @@
 HALF = D // 2
 SUB = 4
 prior_count = 2.0
+X, Y = 4, 8
+ORDER = [[x * Y + y for y in range(Y) for x in range(X)]]
 scale = D ** (-0.5)
 
 f32, bf16 = jnp.float32, jnp.bfloat16
@@ -147,7 +149,8 @@
 def body(embeddings, counts, centroids):
     total, n_cents = embeddings.shape[0], centroids.shape[0]
     n_items, n_split = lax.axis_size("items"), lax.axis_size("cents")
-    place = lax.axis_index("items").astype(jnp.int32)[None]
+    item = lax.axis_index("items").astype(jnp.int32)
+    place = (item % Y * X + item // Y)[None]
     score_shape = pltpu.VMEM((n_cents, total), f32)
     logs_shape = pltpu.VMEM((n_split, 1, total), f32)
     sent_shape = pltpu.VMEM((n_cents // TILE, 2, 2 * HALF // LANES + 1, SUB, LANES), bf16)
@@ -185,7 +188,7 @@
             compiler_params=params(16),
             name="moments",
         )(known, logs, score, rows)
-        parts = lax.all_to_all(sent.reshape(n_items, *sent.shape[2:]), "items", 0, 0)
+        parts = lax.all_to_all(sent.reshape(n_items, *sent.shape[2:]), "items", 0, 0, axis_index_groups=ORDER)
         if step:
             fresh = pl.pallas_call(
                 later_update,
@@ -204,7 +207,7 @@
                 compiler_params=params(16),
                 name="first_update",
             )(known, parts, centroids)
-        blocks = lax.all_to_all(fresh, "items", 0, 0)
+        blocks = lax.all_to_all(fresh, "items", 0, 0, axis_index_groups=ORDER)
         blocks = blocks.reshape(n_cents // TILE, 2, TILE, HALF).transpose(0, 2, 1, 3)
         current = blocks.reshape(n_cents, D)
     return current

time: 114 us -> 112 us (0.982)
  blocking collectives: 106 us -> 104 us
    all_to_all x4, blocking collectives: 75.5 us -> 74.3 us  [the longest x2 41.9 us: body(): lax.all_to_all(sent.reshape(n_items, *sent.shape[2:]), 'items', 0, 0, axi...]
where the time goes in v6:
time: 112 us
  blocking collectives  104 us (93%)
  Pallas kernels  6.36 us (6%)
    all_to_all x2, blocking collectives, body(): lax.all_to_all(sent.reshape(n_items, *sent.shape[2:]), 'items', 0, 0, axi...  41.9 us
    all_to_all x2, blocking collectives, body(): blocks = lax.all_to_all(fresh, 'items', 0, 0, axis_index_groups=ORDER)  32.4 us
    all_to_all x2, blocking collectives, body(): logs = lax.all_to_all(logs, 'cents', 0, 0)  30.1 us
    pallas_call x1, Pallas kernels, body(): pl.pallas_call(first_scores, out_shape=(pltpu.VMEM(embeddings.shape, bf16...  3.12 us

profile of v6, /device:TPU:8, one launch (start us, length us, event | category | flops | bytes accessed | tf_op | source)
XLA Modules:
  0.0 112.2 jit_solution(10464191672911383866)
XLA Ops:
  0.7 3.1 %first_scores.1 = (bf16[1920,1024]{1,0:T(8,128)(2,1)S(1)}, f32[128,1920]{1,0:T(8,128)S(1)}, f32[16,1,1920]{2,1,0:T(1,128)S(1)}, s32[2]{0:T(128)S(4)}) custom-call(s32[1]{0:T(128)S(6)} %copy.5.count_ref, s32[1]{0:T(128)} %bitcast.place_ref, bf16[1920,1024]{1,0:T(8,128)(2,1)} %rows_hbm.1, bf16[128,1024]{1,0:T(8,128)(2,1)} %cents_ref.1), custom_call_target="tpu_custom_call" | custom-call | tf_op jit(solution)/shard_map/first_scores/pallas_call | solution.py:159
  3.8 0.0 copy-start
  3.8 19.0 %all_to_all.30.logs_ref = f32[16,1,1920]{2,1,0:T(1,128)S(1)} all-to-all(f32[16,1,1920]{2,1,0:T(1,128)S(1)} %get-tuple-element.13), channel_id=1, replica_groups=mesh['items'=32,'cents'=16] {'cents'}, dimensions={0} | all-to-all | bytes 245760 | tf_op jit(solution)/shard_map/all_to_all | solution.py:182
  22.8 0.8 moments.2
  23.6 23.7 %all_to_all.31.parts_ref = bf16[32,9,4,128]{3,2,1,0:T(4,128)(2,1)S(1)} all-to-all(bf16[32,9,4,128]{3,2,1,0:T(4,128)(2,1)S(1)} %bitcast.14), channel_id=1, replica_groups={{0,128,256,384,16,144,272,400,32,160,288,416,48,176,304,432,64,192,320,..., dimensions={0} | all-to-all | bytes 589824 | tf_op jit(solution)/shard_map/all_to_all | solution.py:191
  47.2 0.0 copy-done
  47.2 0.2 first_update.1.fresh_ref
  47.4 16.2 %all_to_all.32 = bf16[32,8,512]{2,1,0:T(8,128)(2,1)S(1)} all-to-all(bf16[32,8,512]{2,1,0:T(8,128)(2,1)S(1)} %first_update.1.fresh_ref), channel_id=1, replica_groups={{0,128,256,384,16,144,272,400,32,160,288,416,48,176,304,432,64,192,320,..., dimensions={0} | all-to-all | bytes 524288 | tf_op jit(solution)/shard_map/all_to_all | solution.py:210
  63.7 1.3 %later_scores.1 = (f32[128,1920]{1,0:T(8,128)S(1)}, f32[16,1,1920]{2,1,0:T(1,128)S(1)}) custom-call(bf16[1920,1024]{1,0:T(8,128)(2,1)S(1)} %get-tuple-element.12.rows_ref, bf16[128,1024]{1,0:T(8,128)(2,1)S(1)} %bitcast.15), custom_call_target="tpu_custom_call" | custom-call | tf_op jit(solution)/shard_map/later_scores/pallas_call | solution.py:174
  64.9 11.2 %all_to_all.33.logs_ref = f32[16,1,1920]{2,1,0:T(1,128)S(1)} all-to-all(f32[16,1,1920]{2,1,0:T(1,128)S(1)} %get-tuple-element.15), channel_id=1, replica_groups=mesh['items'=32,'cents'=16] {'cents'}, dimensions={0} | all-to-all | bytes 245760 | tf_op jit(solution)/shard_map/all_to_all | solution.py:182
  76.1 0.8 moments.3
  76.9 18.2 %all_to_all.34.parts_ref = bf16[32,9,4,128]{3,2,1,0:T(4,128)(2,1)S(1)} all-to-all(bf16[32,9,4,128]{3,2,1,0:T(4,128)(2,1)S(1)} %bitcast.13), channel_id=1, replica_groups={{0,128,256,384,16,144,272,400,32,160,288,416,48,176,304,432,64,192,320,..., dimensions={0} | all-to-all | bytes 589824 | tf_op jit(solution)/shard_map/all_to_all | solution.py:191
  95.1 0.2 later_update.1
  95.3 16.2 %all_to_all.35 = bf16[32,8,512]{2,1,0:T(8,128)(2,1)S(1)} all-to-all(bf16[32,8,512]{2,1,0:T(8,128)(2,1)S(1)} %later_update.1), channel_id=1, replica_groups={{0,128,256,384,16,144,272,400,32,160,288,416,48,176,304,432,64,192,320,..., dimensions={0} | all-to-all | bytes 524288 | tf_op jit(solution)/shard_map/all_to_all | solution.py:210
  111.5 0.7 copy.6
Async XLA Ops:
  3.8 43.4 %copy-start = (bf16[128,1024]{1,0:T(8,128)(2,1)S(1)}, bf16[128,1024]{1,0:T(8,128)(2,1)}, u32[]{:S(2)}) copy-start(bf16[128,1024]{1,0:T(8,128)(2,1)} %cents_ref.1) | copy-start | bytes 786436

commit v7 on v6

--- a/solution.py
+++ b/solution.py
@@ -17,6 +17,8 @@
 prior_count = 2.0
 X, Y = 4, 8
 ORDER = [[x * Y + y for y in range(Y) for x in range(X)]]
+Z, CORE = 8, 2
+CENT_ORDER = [[z * CORE + core for core in range(CORE) for z in range(Z)]]
 scale = D ** (-0.5)
 
 f32, bf16 = jnp.float32, jnp.bfloat16
@@ -179,7 +181,7 @@
                 compiler_params=params(16),
                 name="later_scores",
             )(rows, current)
-        logs = lax.all_to_all(logs, "cents", 0, 0)
+        logs = lax.all_to_all(logs, "cents", 0, 0, axis_index_groups=CENT_ORDER)
         sent = pl.pallas_call(
             moments,
             out_shape=sent_shape,

time: 112 us -> 109 us (0.973)
  the two profiles are of different devices: /device:TPU:8 before, /device:TPU:64 now
where the time goes in v7:
time: 109 us
  blocking collectives  101 us (93%)
  Pallas kernels  6.36 us (6%)
    all_to_all x2, blocking collectives, body(): lax.all_to_all(sent.reshape(n_items, *sent.shape[2:]), 'items', 0, 0, axi...  39 us
    all_to_all x2, blocking collectives, body(): blocks = lax.all_to_all(fresh, 'items', 0, 0, axis_index_groups=ORDER)  32.3 us
    all_to_all x2, blocking collectives, body(): logs = lax.all_to_all(logs, 'cents', 0, 0, axis_index_groups=CENT_ORDER)  30.1 us
    pallas_call x1, Pallas kernels, body(): pl.pallas_call(first_scores, out_shape=(pltpu.VMEM(embeddings.shape, bf16...  3.12 us

profile of v7, /device:TPU:64, one launch (start us, length us, event | category | flops | bytes accessed | tf_op | source)
XLA Modules:
  0.0 109.2 jit_solution(15915824127198121175)
XLA Ops:
  0.7 3.1 %first_scores.1 = (bf16[1920,1024]{1,0:T(8,128)(2,1)S(1)}, f32[128,1920]{1,0:T(8,128)S(1)}, f32[16,1,1920]{2,1,0:T(1,128)S(1)}, s32[2]{0:T(128)S(4)}) custom-call(s32[1]{0:T(128)S(6)} %copy.5.count_ref, s32[1]{0:T(128)} %bitcast.place_ref, bf16[1920,1024]{1,0:T(8,128)(2,1)} %rows_hbm.1, bf16[128,1024]{1,0:T(8,128)(2,1)} %cents_ref.1), custom_call_target="tpu_custom_call" | custom-call | tf_op jit(solution)/shard_map/first_scores/pallas_call | solution.py:161
  3.8 0.0 copy-start
  3.8 18.0 %all_to_all.30.logs_ref = f32[16,1,1920]{2,1,0:T(1,128)S(1)} all-to-all(f32[16,1,1920]{2,1,0:T(1,128)S(1)} %get-tuple-element.13), channel_id=1, replica_groups={{0,2,4,6,8,10,12,14,1,3,5,7,9,11,13,15},{16,18,20,22,24,26,28,30,17,19,..., dimensions={0} | all-to-all | bytes 245760 | tf_op jit(solution)/shard_map/all_to_all | solution.py:184
  21.8 0.8 moments.2
  22.6 22.6 %all_to_all.31.parts_ref = bf16[32,9,4,128]{3,2,1,0:T(4,128)(2,1)S(1)} all-to-all(bf16[32,9,4,128]{3,2,1,0:T(4,128)(2,1)S(1)} %bitcast.14), channel_id=1, replica_groups={{0,128,256,384,16,144,272,400,32,160,288,416,48,176,304,432,64,192,320,..., dimensions={0} | all-to-all | bytes 589824 | tf_op jit(solution)/shard_map/all_to_all | solution.py:193
  45.2 0.0 copy-done
  45.2 0.2 first_update.1.fresh_ref
  45.4 16.1 %all_to_all.32 = bf16[32,8,512]{2,1,0:T(8,128)(2,1)S(1)} all-to-all(bf16[32,8,512]{2,1,0:T(8,128)(2,1)S(1)} %first_update.1.fresh_ref), channel_id=1, replica_groups={{0,128,256,384,16,144,272,400,32,160,288,416,48,176,304,432,64,192,320,..., dimensions={0} | all-to-all | bytes 524288 | tf_op jit(solution)/shard_map/all_to_all | solution.py:212
  61.5 1.3 %later_scores.1 = (f32[128,1920]{1,0:T(8,128)S(1)}, f32[16,1,1920]{2,1,0:T(1,128)S(1)}) custom-call(bf16[1920,1024]{1,0:T(8,128)(2,1)S(1)} %get-tuple-element.12.rows_ref, bf16[128,1024]{1,0:T(8,128)(2,1)S(1)} %bitcast.15), custom_call_target="tpu_custom_call" | custom-call | tf_op jit(solution)/shard_map/later_scores/pallas_call | solution.py:176
  62.8 12.1 %all_to_all.33.logs_ref = f32[16,1,1920]{2,1,0:T(1,128)S(1)} all-to-all(f32[16,1,1920]{2,1,0:T(1,128)S(1)} %get-tuple-element.15), channel_id=1, replica_groups={{0,2,4,6,8,10,12,14,1,3,5,7,9,11,13,15},{16,18,20,22,24,26,28,30,17,19,..., dimensions={0} | all-to-all | bytes 245760 | tf_op jit(solution)/shard_map/all_to_all | solution.py:184
  74.9 0.8 moments.3
  75.7 16.4 %all_to_all.34.parts_ref = bf16[32,9,4,128]{3,2,1,0:T(4,128)(2,1)S(1)} all-to-all(bf16[32,9,4,128]{3,2,1,0:T(4,128)(2,1)S(1)} %bitcast.13), channel_id=1, replica_groups={{0,128,256,384,16,144,272,400,32,160,288,416,48,176,304,432,64,192,320,..., dimensions={0} | all-to-all | bytes 589824 | tf_op jit(solution)/shard_map/all_to_all | solution.py:193
  92.1 0.2 later_update.1
  92.3 16.1 %all_to_all.35 = bf16[32,8,512]{2,1,0:T(8,128)(2,1)S(1)} all-to-all(bf16[32,8,512]{2,1,0:T(8,128)(2,1)S(1)} %later_update.1), channel_id=1, replica_groups={{0,128,256,384,16,144,272,400,32,160,288,416,48,176,304,432,64,192,320,..., dimensions={0} | all-to-all | bytes 524288 | tf_op jit(solution)/shard_map/all_to_all | solution.py:212
  108.5 0.7 copy.6
Async XLA Ops:
  3.8 41.4 %copy-start = (bf16[128,1024]{1,0:T(8,128)(2,1)S(1)}, bf16[128,1024]{1,0:T(8,128)(2,1)}, u32[]{:S(2)}) copy-start(bf16[128,1024]{1,0:T(8,128)(2,1)} %cents_ref.1) | copy-start | bytes 786436

commit v8 on v7

--- a/solution.py
+++ b/solution.py
@@ -16,7 +16,7 @@
 SUB = 4
 prior_count = 2.0
 X, Y = 4, 8
-ORDER = [[x * Y + y for y in range(Y) for x in range(X)]]
+ORDER = [[x * Y + y for y in range(Y) for x in (0, 2, 1, 3)]]
 Z, CORE = 8, 2
 CENT_ORDER = [[z * CORE + core for core in range(CORE) for z in range(Z)]]
 scale = D ** (-0.5)
@@ -152,7 +152,8 @@
     total, n_cents = embeddings.shape[0], centroids.shape[0]
     n_items, n_split = lax.axis_size("items"), lax.axis_size("cents")
     item = lax.axis_index("items").astype(jnp.int32)
-    place = (item % Y * X + item // Y)[None]
+    x = item // Y
+    place = (item % Y * X + x // 2 + x % 2 * 2)[None]
     score_shape = pltpu.VMEM((n_cents, total), f32)
     logs_shape = pltpu.VMEM((n_split, 1, total), f32)
     sent_shape = pltpu.VMEM((n_cents // TILE, 2, 2 * HALF // LANES + 1, SUB, LANES), bf16)

time: 109 us -> 109 us (level)
  no operation moved by 1% of the time
where the time goes in v8:
time: 109 us
  blocking collectives  101 us (93%)
  Pallas kernels  6.36 us (6%)
    all_to_all x2, blocking collectives, body(): lax.all_to_all(sent.reshape(n_items, *sent.shape[2:]), 'items', 0, 0, axi...  38.9 us
    all_to_all x2, blocking collectives, body(): blocks = lax.all_to_all(fresh, 'items', 0, 0, axis_index_groups=ORDER)  32.3 us
    all_to_all x2, blocking collectives, body(): logs = lax.all_to_all(logs, 'cents', 0, 0, axis_index_groups=CENT_ORDER)  30 us
    pallas_call x1, Pallas kernels, body(): pl.pallas_call(first_scores, out_shape=(pltpu.VMEM(embeddings.shape, bf16...  3.12 us

profile of v8, /device:TPU:64, one launch (start us, length us, event | category | flops | bytes accessed | tf_op | source)
XLA Modules:
  0.0 109.0 jit_solution(3885310349435707146)
XLA Ops:
  0.7 3.1 %first_scores.1 = (bf16[1920,1024]{1,0:T(8,128)(2,1)S(1)}, f32[128,1920]{1,0:T(8,128)S(1)}, f32[16,1,1920]{2,1,0:T(1,128)S(1)}, s32[2]{0:T(128)S(4)}) custom-call(s32[1]{0:T(128)S(6)} %copy.5.count_ref, s32[1]{0:T(128)} %bitcast.place_ref, bf16[1920,1024]{1,0:T(8,128)(2,1)} %rows_hbm.1, bf16[128,1024]{1,0:T(8,128)(2,1)} %cents_ref.1), custom_call_target="tpu_custom_call" | custom-call | tf_op jit(solution)/shard_map/first_scores/pallas_call | solution.py:162
  3.8 0.0 copy-start
  3.8 18.0 %all_to_all.30.logs_ref = f32[16,1,1920]{2,1,0:T(1,128)S(1)} all-to-all(f32[16,1,1920]{2,1,0:T(1,128)S(1)} %get-tuple-element.13), channel_id=1, replica_groups={{0,2,4,6,8,10,12,14,1,3,5,7,9,11,13,15},{16,18,20,22,24,26,28,30,17,19,..., dimensions={0} | all-to-all | bytes 245760 | tf_op jit(solution)/shard_map/all_to_all | solution.py:185
  21.8 0.8 moments.2
  22.6 22.6 %all_to_all.31.parts_ref = bf16[32,9,4,128]{3,2,1,0:T(4,128)(2,1)S(1)} all-to-all(bf16[32,9,4,128]{3,2,1,0:T(4,128)(2,1)S(1)} %bitcast.14), channel_id=1, replica_groups={{0,256,128,384,16,272,144,400,32,288,160,416,48,304,176,432,64,320,192,..., dimensions={0} | all-to-all | bytes 589824 | tf_op jit(solution)/shard_map/all_to_all | solution.py:194
  45.2 0.0 copy-done
  45.2 0.2 first_update.1.fresh_ref
  45.4 16.1 %all_to_all.32 = bf16[32,8,512]{2,1,0:T(8,128)(2,1)S(1)} all-to-all(bf16[32,8,512]{2,1,0:T(8,128)(2,1)S(1)} %first_update.1.fresh_ref), channel_id=1, replica_groups={{0,256,128,384,16,272,144,400,32,288,160,416,48,304,176,432,64,320,192,..., dimensions={0} | all-to-all | bytes 524288 | tf_op jit(solution)/shard_map/all_to_all | solution.py:213
  61.5 1.3 %later_scores.1 = (f32[128,1920]{1,0:T(8,128)S(1)}, f32[16,1,1920]{2,1,0:T(1,128)S(1)}) custom-call(bf16[1920,1024]{1,0:T(8,128)(2,1)S(1)} %get-tuple-element.12.rows_ref, bf16[128,1024]{1,0:T(8,128)(2,1)S(1)} %bitcast.15), custom_call_target="tpu_custom_call" | custom-call | tf_op jit(solution)/shard_map/later_scores/pallas_call | solution.py:177
  62.8 12.0 %all_to_all.33.logs_ref = f32[16,1,1920]{2,1,0:T(1,128)S(1)} all-to-all(f32[16,1,1920]{2,1,0:T(1,128)S(1)} %get-tuple-element.15), channel_id=1, replica_groups={{0,2,4,6,8,10,12,14,1,3,5,7,9,11,13,15},{16,18,20,22,24,26,28,30,17,19,..., dimensions={0} | all-to-all | bytes 245760 | tf_op jit(solution)/shard_map/all_to_all | solution.py:185
  74.9 0.8 moments.3
  75.7 16.3 %all_to_all.34.parts_ref = bf16[32,9,4,128]{3,2,1,0:T(4,128)(2,1)S(1)} all-to-all(bf16[32,9,4,128]{3,2,1,0:T(4,128)(2,1)S(1)} %bitcast.13), channel_id=1, replica_groups={{0,256,128,384,16,272,144,400,32,288,160,416,48,304,176,432,64,320,192,..., dimensions={0} | all-to-all | bytes 589824 | tf_op jit(solution)/shard_map/all_to_all | solution.py:194
  91.9 0.2 later_update.1
  92.2 16.1 %all_to_all.35 = bf16[32,8,512]{2,1,0:T(8,128)(2,1)S(1)} all-to-all(bf16[32,8,512]{2,1,0:T(8,128)(2,1)S(1)} %later_update.1), channel_id=1, replica_groups={{0,256,128,384,16,272,144,400,32,288,160,416,48,304,176,432,64,320,192,..., dimensions={0} | all-to-all | bytes 524288 | tf_op jit(solution)/shard_map/all_to_all | solution.py:213
  108.3 0.7 copy.6
Async XLA Ops:
  3.8 41.4 %copy-start = (bf16[128,1024]{1,0:T(8,128)(2,1)S(1)}, bf16[128,1024]{1,0:T(8,128)(2,1)}, u32[]{:S(2)}) copy-start(bf16[128,1024]{1,0:T(8,128)(2,1)} %cents_ref.1) | copy-start | bytes 786436
